TPU v7x, 512 devices: a whole 4x8x8 slice. The times are simulated.
512 devices in a mesh: dp: 2 (over core), seq: 64 (over y, z), tensor: 4 (over x).
Axes of the slice: x: 4, y: 8, z: 8, core: 2. Of those that a mesh axis runs over, the one named last changes fastest.
Arguments:
- query: bfloat16 [2, 16384, 2048], P('dp', 'seq', 'tensor'), may hold values from -1.75 to 1.75
- key_rows: bfloat16 [2, 16384, 2048], P('dp', 'seq', 'tensor'), may hold values from -1.75 to 1.75
- value: bfloat16 [2, 16384, 2048], P('dp', 'seq', 'tensor'), may hold values from -40 to 40
- gain: float32 [2048], P('tensor'), may hold values from 0.25 to 1.75
- grad_out: bfloat16 [2, 16384, 2048], P('dp', 'seq', 'tensor'), may hold values from -16 to 16
- start_offset: int32 [2, 256], P('dp', 'seq'), may hold values from 0 to 64, as said below
Outputs:
- attn_out: bfloat16 [2, 16384, 2048], P('dp', 'seq', 'tensor')
- grad_query: bfloat16 [2, 16384, 2048], P('dp', 'seq', 'tensor')
- grad_key: bfloat16 [2, 16384, 2048], P('dp', 'seq', 'tensor')
- grad_value: bfloat16 [2, 16384, 2048], P('dp', 'seq', 'tensor')
- grad_gain: float32 [2048], P('tensor')
Inputs may be any that keep to these rules, and one draw needn't show every extreme that they name: `start_offset`: the position within its block of 64 positions at which a document starts; 64 when none starts in the block; every sequence begins a document at its first position.
All inputs are finite; a program needn't handle non-finite values.
Results may differ from a plain program's by a relative error of at most 0.0058.
Values sent between devices are 32-bit elements; how exact they have to be, the bound alone decides.
No kernel may reach another device: no remote copies, remote signals or barrier semaphores. Data moves between devices by JAX's collectives and lax.ppermute only.
A program may use at most 64 MiB of HBM per device.

v0:
```python
import jax
import jax.numpy as jnp
from jax import lax
from jax.sharding import PartitionSpec as P

DH = 128
BLK = 64
CH = 2048


eps_value = 1e-05


def carried_in(part, axis, combine, identity, reverse):
    count = lax.axis_size(axis)
    place = lax.axis_index(axis)
    ahead = count - 1 - place if reverse else place
    gathered = jax.tree.map(lambda a: lax.all_gather(a, axis), part)
    state = jax.tree.map(lambda a, e: jnp.zeros_like(a) + jnp.asarray(e, a.dtype), part, identity)

    def one(turn, state):
        source = count - 1 - turn if reverse else turn
        return combine(
            state, jax.tree.map(lambda a: lax.dynamic_index_in_dim(a, source, 0, False), gathered)
        )

    return lax.fori_loop(0, ahead, one, state)


def segment_rows(offsets, length_dev):
    positions = jnp.arange(length_dev, dtype=jnp.int32)
    block_starts = jnp.arange(offsets.shape[0], dtype=jnp.int32) * BLK + offsets
    present = offsets < BLK
    covered = (block_starts[None, :] <= positions[:, None]) & present[None, :]
    labels = jnp.sum(covered.astype(jnp.int32), axis=1)
    allowed = (labels[:, None] == labels[None, :]) & (positions[None, :] <= positions[:, None])
    starts = jnp.sum(present.astype(jnp.int32))
    return (labels, starts, allowed)


def joined(earlier, later):
    return (
        jnp.where(later[1] > 0, later[0], earlier[0] + later[0]),
        jnp.maximum(earlier[1], later[1]),
    )


def shards(query, key_rows, value, gain, grad_out, start_offset):
    length_dev = query.shape[1]
    width_local = query.shape[2]
    heads_local = width_local // DH
    query_heads = query[0].reshape(length_dev, heads_local, DH)
    key_heads = key_rows[0].reshape(length_dev, heads_local, DH)
    value_heads = value[0].reshape(length_dev, heads_local, DH)
    labels, starts, allowed = segment_rows(start_offset[0], length_dev)
    head_mask = (labels == 0)[:, None, None]
    tail_mask = (labels == starts)[:, None, None]
    reset = (starts > 0).astype(jnp.int32)
    scores = jnp.einsum("thd,shd->hts", query_heads, key_heads, preferred_element_type=jnp.float32)
    weights = jnp.where(allowed[None], scores, 0.0).astype(jnp.bfloat16)
    local_out = jnp.einsum("hts,shd->thd", weights, value_heads, preferred_element_type=jnp.float32)
    tail_keys = jnp.where(tail_mask, key_heads, jnp.zeros_like(key_heads))
    tail_values = jnp.where(tail_mask, value_heads, jnp.zeros_like(value_heads))
    tail_state = jnp.einsum(
        "shi,shj->hij", tail_keys, value_heads, preferred_element_type=jnp.float32
    )
    zero_state = jnp.zeros_like(tail_state)
    incoming = carried_in((tail_state, reset), "seq", joined, (zero_state, jnp.int32(0)), False)[0]
    carried = incoming.astype(jnp.bfloat16)
    head_query = jnp.where(head_mask, query_heads, jnp.zeros_like(query_heads))
    carried_out = jnp.einsum(
        "thi,hij->thj", head_query, carried, preferred_element_type=jnp.float32
    )
    attended = (local_out + carried_out).reshape(length_dev, width_local)
    upstream = grad_out[0].astype(jnp.float32)
    scaled = gain[None, :] * upstream
    square_local = jnp.sum(attended * attended, axis=1)
    square_total = lax.psum(square_local, "tensor")
    inverse = lax.rsqrt(square_total / CH + eps_value)
    normed = attended * inverse[:, None]
    product_total = lax.psum(jnp.sum(scaled * normed, axis=1), "tensor")
    output = (gain[None, :] * normed).astype(jnp.bfloat16)
    grad_pre = (inverse[:, None] * (scaled - normed * (product_total / CH)[:, None])).astype(
        jnp.bfloat16
    )
    gain_local = jnp.sum(upstream * normed, axis=0)
    grad_gain = lax.psum(gain_local, ("dp", "seq"))
    grad_heads = grad_pre.reshape(length_dev, heads_local, DH)
    grad_state = jnp.einsum(
        "thi,thj->hij", head_query, grad_heads, preferred_element_type=jnp.float32
    )
    later = carried_in((grad_state, reset), "seq", joined, (zero_state, jnp.int32(0)), True)[0]
    later_half = later.astype(jnp.bfloat16)
    grad_scores = jnp.einsum(
        "thd,shd->hts", grad_heads, value_heads, preferred_element_type=jnp.float32
    )
    grad_weights = jnp.where(allowed[None], grad_scores, 0.0).astype(jnp.bfloat16)
    head_grad = jnp.where(head_mask, grad_heads, jnp.zeros_like(grad_heads))
    grad_query = jnp.einsum(
        "hts,shd->thd", grad_weights, key_heads, preferred_element_type=jnp.float32
    ) + jnp.einsum("thj,hij->thi", head_grad, carried, preferred_element_type=jnp.float32)
    grad_key = jnp.einsum(
        "hts,thd->shd", grad_weights, query_heads, preferred_element_type=jnp.float32
    ) + jnp.einsum("shj,hij->shi", tail_values, later_half, preferred_element_type=jnp.float32)
    grad_value = jnp.einsum(
        "hts,thd->shd", weights, grad_heads, preferred_element_type=jnp.float32
    ) + jnp.einsum("shi,hij->shj", tail_keys, later_half, preferred_element_type=jnp.float32)
    shape_dev = (1, length_dev, width_local)
    return (
        output.reshape(shape_dev),
        grad_query.reshape(shape_dev).astype(jnp.bfloat16),
        grad_key.reshape(shape_dev).astype(jnp.bfloat16),
        grad_value.reshape(shape_dev).astype(jnp.bfloat16),
        grad_gain,
    )


def solution(mesh):
    return jax.shard_map(
        shards,
        mesh=mesh,
        in_specs=(
            P("dp", "seq", "tensor"),
            P("dp", "seq", "tensor"),
            P("dp", "seq", "tensor"),
            P("tensor"),
            P("dp", "seq", "tensor"),
            P("dp", "seq"),
        ),
        out_specs=(
            P("dp", "seq", "tensor"),
            P("dp", "seq", "tensor"),
            P("dp", "seq", "tensor"),
            P("dp", "seq", "tensor"),
            P("tensor"),
        ),
        check_vma=False,
    )
```

profile of v0, /device:TPU:2, one launch (start us, length us, event | category | flops | bytes accessed | tf_op | source)
XLA Modules:
  0.0 734.2 jit_solution(13396427716960763037)
XLA Ops:
  7.9 1.3 fusion.29
  9.2 1.1 copy.54
  10.3 1.1 copy.57
  13.8 1.1 copy.53
  14.9 1.1 copy.62
  15.9 1.3 dynamic-slice
  18.0 31.0 %all-reduce = s32[64]{0:T(128)S(1)} all-reduce(s32[64]{0:T(128)S(1)} %dynamic-update-slice), channel_id=1, replica_groups=mesh['dp'=2,'seq'=64,'tensor'=4] {'seq'}, use_global_device_ids=true, to_apply=%add | all-reduce | flops 64 | bytes 512
  49.8 107.7 %all-gather.5.cloned.1.call-done = f32[256,128,128]{2,1,0:T(8,128)} async-done(((f32[4,128,128]{2,1,0:T(8,128)}), f32[256,128,128]{2,1,0:T(8,128)}) %all-gather.5.cloned.1.call-update) | async-done | bytes 16777232 | tf_op jit(solution)/shard_map/all_gather | solution.py:18
  157.8 8.6 %psum.21 = f32[256]{0:T(256)S(1)} all-reduce(f32[256]{0:T(256)S(1)} %get-tuple-element.176), channel_id=1, replica_groups=mesh['dp'=2,'seq'=64,'tensor'=4] {'tensor'}, use_global_device_ids=true, to_apply=%region_5.6 | all-reduce | flops 256 | bytes 2048 | tf_op jit(solution)/shard_map/psum | solution.py:78
  166.6 1.2 fusion.10
  167.8 10.1 %psum.22 = f32[256]{0:T(256)S(1)} all-reduce(f32[256]{0:T(256)S(1)} %get-tuple-element.151), channel_id=1, replica_groups=mesh['dp'=2,'seq'=64,'tensor'=4] {'tensor'}, use_global_device_ids=true, to_apply=%region_7.8 | all-reduce | flops 256 | bytes 2048 | tf_op jit(solution)/shard_map/psum | solution.py:81
  181.7 396.3 %psum.23 = f32[512]{0:T(512)} all-reduce(f32[512]{0:T(512)S(1)} %get-tuple-element.150), channel_id=1, replica_groups=mesh['dp'=2,'seq'=64,'tensor'=4] {'dp','seq'}, use_global_device_ids=true, to_apply=%region_11.12 | all-reduce | flops 512 | bytes 4096 | tf_op jit(solution)/shard_map/psum | solution.py:87
  579.3 145.9 %while.27 = (s32[]{:T(128)}, f32[4,128,128]{2,1,0:T(8,128)S(1)}, s32[]{:T(128)}, s32[64]{0:T(128)S(1)}, f32[64,4,128,128]{3,2,1,0:T(8,128)}, /*index=5*/s32[]{:T(128)}, s32[]{:T(128)}, s32[]{:T(128)}, s32[]{:T(128)}, s32[1]{0:T(128)}) while((s32[]{:T(128)}, f32[4,128,128]{2,1,0:T(8,128)S(1)}, s32[]{:T(128)}, s32[64]{0:T(128)S(1)}, ...), condition=%wide.region_9.10_spmd, body=%wide.region_8.9_spmd.sunk | while | flops 131079 | bytes 786613 | solution.py:27
  582.9 1.1 add_select_fusion.5
  587.5 1.1 add_select_fusion.5
  592.1 1.1 add_select_fusion.5
  596.8 1.1 add_select_fusion.5
  599.1 1.1 add_select_fusion.5
  601.4 1.1 add_select_fusion.5
  603.7 1.1 add_select_fusion.5
  606.0 1.1 add_select_fusion.5
  608.3 1.1 add_select_fusion.5
  613.0 1.1 add_select_fusion.5
  617.6 1.1 add_select_fusion.5
  (152 shorter events, 103.4 us)
Async XLA Ops:
  7.2 570.8 %copy-start = (f32[512]{0:T(512)S(1)}, f32[512]{0:T(512)}, u32[]{:S(2)}) copy-start(f32[512]{0:T(512)} %param.13) | copy-start | bytes 6148
  7.2 150.3 %all-gather.5.cloned.1.call-start = ((), (), s32[]{:S(2)}) async-start(), calls=%async_computation | async-start | bytes 17039360 | tf_op jit(solution)/shard_map/all_gather | solution.py:18
  13.1 566.2 %all-gather.7.cloned.1.call-start = ((), (), s32[]{:S(2)}) async-start(), calls=%async_computation.1 | async-start | bytes 17039360 | tf_op jit(solution)/shard_map/all_gather | solution.py:18
Sparse Core Ops, SparseCore 0:
  13.2 144.2 all-gather.4
  179.9 279.8 all-gather.6
where the time goes:
time: 743 us; the launch traced here: 734 us
  blocking collectives  446 us (60%)
  waiting for transfers between devices  108 us (15%)
  other arithmetic  71.9 us (10%)
  local copies, waits for them, and re-layouts  46.4 us (6%)
  loops' own time  42.6 us (6%)
  between operations  14.9 us (2%)
    psum x1, blocking collectives, shards(): grad_gain = lax.psum(gain_local, ('dp', 'seq'))  396 us
    all_gather x2, waiting for transfers between devices, carried_in(): gathered = jax.tree.map(lambda a: lax.all_gather(a, axis), part)  108 us
    select_n x63, other arithmetic, joined(): jnp.where(later[1] > 0, later[0], earlier[0] + later[0])  66.2 us
    another operation x2, loops' own time, carried_in(): return lax.fori_loop(0, ahead, one, state)  42.6 us
    dynamic_slice x63, local copies, waits for them, and re-layouts, one(): lax.dynamic_index_in_dim(a, source, 0, False)  37.1 us
    unnamed x1, blocking collectives  31 us
  transfers between devices with their start and end apart: 2, of which 1 were waited for; matrix products, arithmetic and copies ran while one was open for 1% of the time, Pallas kernels for 0%

commit v1 on v0

v1 whole, which is shorter than its diff:
```python
import jax
import jax.numpy as jnp
from jax import lax
from jax.experimental import pallas as pl
from jax.experimental.pallas import tpu as pltpu
from jax.sharding import PartitionSpec as P

DH = 128
BLK = 64
CH = 2048
EPS = 1e-05
VMEM = pl.BlockSpec(memory_space=pltpu.VMEM)
SMEM = pl.BlockSpec(memory_space=pltpu.SMEM)
F32 = jnp.float32
BF16 = jnp.bfloat16


def dot(a, b, ca, cb):
    return lax.dot_general(a, b, (((ca,), (cb,)), ((), ())), preferred_element_type=F32)


def bounds(off_ref):
    first, last, count = jnp.int32(1 << 20), jnp.int32(-1), jnp.int32(0)
    for b in range(off_ref.shape[1]):
        off = off_ref[0, b]
        present = off < BLK
        first = jnp.minimum(first, jnp.where(present, b * BLK + off, 1 << 20))
        last = jnp.maximum(last, jnp.where(present, b * BLK + off, -1))
        count += present.astype(jnp.int32)
    return first, last, count


def labels_of(off_ref, pos):
    labels = jnp.zeros(pos.shape, jnp.int32)
    for b in range(off_ref.shape[1]):
        off = off_ref[0, b]
        start = jnp.where(off < BLK, b * BLK + off, 1 << 20)
        labels += (pos >= start).astype(jnp.int32)
    return labels


def allowed_of(off_ref, length):
    t = lax.broadcasted_iota(jnp.int32, (length, length), 0)
    s = lax.broadcasted_iota(jnp.int32, (length, length), 1)
    rows = labels_of(off_ref, lax.broadcasted_iota(jnp.int32, (length, 1), 0))
    cols = labels_of(off_ref, lax.broadcasted_iota(jnp.int32, (1, length), 1))
    return (rows == cols) & (s <= t)


def row_mask(length, first=None, last=None):
    pos = lax.broadcasted_iota(jnp.int32, (length, DH), 0)
    return pos < first if last is None else pos >= last


def put_slices(send_ref, h, state):
    for j in range(DH // 8):
        at = 9 * (h * (DH // 8) + j)
        send_ref[at : at + 8, :] = state[8 * j : 8 * j + 8, :]


def head(h):
    return slice(h * DH, (h + 1) * DH)


def tail_kernel(off_ref, k_ref, v_ref, send_ref):
    length, width = k_ref.shape
    _, last, count = bounds(off_ref)
    tail = row_mask(length, last=last)
    for h in range(width // DH):
        keys = jnp.where(tail, k_ref[:, head(h)], jnp.zeros((), BF16))
        put_slices(send_ref, h, dot(keys, v_ref[:, head(h)], 0, 0))
    keep = jnp.full((1, DH), jnp.where(count > 0, 0.0, 1.0), F32)
    for j in range(send_ref.shape[0] // 9):
        send_ref[9 * j + 8 : 9 * j + 9, :] = keep


def local_kernel(off_ref, q_ref, k_ref, v_ref, out_ref):
    length, width = q_ref.shape
    allowed = allowed_of(off_ref, length)
    for h in range(width // DH):
        scores = dot(q_ref[:, head(h)], k_ref[:, head(h)], 1, 1)
        weights = jnp.where(allowed, scores, 0.0).astype(BF16)
        out_ref[:, head(h)] = dot(weights, v_ref[:, head(h)], 1, 0)


def prefix_kernel(recv_ref, send_ref):
    carry = jnp.zeros((8, DH), F32)
    for w in range(recv_ref.shape[0] // 9):
        send_ref[8 * w : 8 * w + 8, :] = carry
        keep = jnp.broadcast_to(recv_ref[9 * w + 8 : 9 * w + 9, :], (8, DH))
        carry = recv_ref[9 * w : 9 * w + 8, :] + carry * keep


def attend_kernel(off_ref, q_ref, local_ref, state_ref, g_ref, gain_ref, att_ref, sums_ref):
    length, width = q_ref.shape
    first, _, _ = bounds(off_ref)
    opened = row_mask(length, first=first)
    squares = jnp.zeros((length, DH), F32)
    products = jnp.zeros((length, DH), F32)
    for h in range(width // DH):
        query = jnp.where(opened, q_ref[:, head(h)], jnp.zeros((), BF16))
        carried = state_ref[h * DH : (h + 1) * DH, :].astype(BF16)
        att = local_ref[:, head(h)] + dot(query, carried, 1, 0)
        att_ref[:, head(h)] = att
        squares += att * att
        products += (gain_ref[:, head(h)] * g_ref[:, head(h)].astype(F32)) * att
    row = 0
    for total in (squares, products):
        for half in range(length // DH):
            line = jnp.sum(total[half * DH : (half + 1) * DH, :].T, axis=0, keepdims=True)
            for c in range(4):
                sums_ref[4 * c + row : 4 * c + row + 1, :] = line
            row += 1


def norm_kernel(off_ref, q_ref, att_ref, g_ref, gain_ref, sums_ref, out_ref, pre_ref, send_ref):
    length, width = q_ref.shape
    first, _, _ = bounds(off_ref)
    opened = row_mask(length, first=first)
    total = sums_ref[0:4, :] + sums_ref[4:8, :] + sums_ref[8:12, :] + sums_ref[12:16, :]
    halves = length // DH
    inverses, means = [], []
    for half in range(halves):
        inv = lax.rsqrt(total[half : half + 1, :] / CH + EPS)
        mean = inv * total[halves + half : halves + half + 1, :] / CH
        inverses.append(jnp.broadcast_to(inv, (DH, DH)).T)
        means.append(jnp.broadcast_to(mean, (DH, DH)).T)
    inverse = jnp.concatenate(inverses, axis=0)
    mean = jnp.concatenate(means, axis=0)
    zero = jnp.zeros((1, DH), F32)
    for j in range(width // DH, send_ref.shape[0] // 9):
        send_ref[9 * j + 8 : 9 * j + 9, :] = zero
    for h in range(width // DH):
        upstream = g_ref[:, head(h)].astype(F32)
        gain = gain_ref[:, head(h)]
        normed = att_ref[:, head(h)] * inverse
        out_ref[:, head(h)] = (gain * normed).astype(BF16)
        pre = (inverse * (gain * upstream - normed * mean)).astype(BF16)
        pre_ref[:, head(h)] = pre
        send_ref[9 * h + 8 : 9 * h + 9, :] = jnp.sum(upstream * normed, axis=0, keepdims=True)
        query = jnp.where(opened, q_ref[:, head(h)], jnp.zeros((), BF16))
        put_slices(send_ref, h, dot(query, pre, 0, 0))


def suffix_kernel(flags_ref, recv_ref, send_ref):
    count = recv_ref.shape[0] // 9
    carry = jnp.zeros((8, DH), F32)
    total = jnp.zeros((1, DH), F32)
    for w in reversed(range(count)):
        send_ref[9 * w : 9 * w + 8, :] = carry
        keep = jnp.broadcast_to(flags_ref[9 * w + 8 : 9 * w + 9, :], (8, DH))
        carry = recv_ref[9 * w : 9 * w + 8, :] + carry * keep
        total += recv_ref[9 * w + 8 : 9 * w + 9, :]
    for w in range(count):
        send_ref[9 * w + 8 : 9 * w + 9, :] = total


def grads_kernel(off_ref, q_ref, k_ref, v_ref, pre_ref, state_ref, gq_ref, gk_ref, gv_ref):
    length, width = q_ref.shape
    first, _, _ = bounds(off_ref)
    opened = row_mask(length, first=first)
    allowed = allowed_of(off_ref, length)
    for h in range(width // DH):
        query, key, value, pre = (r[:, head(h)] for r in (q_ref, k_ref, v_ref, pre_ref))
        scores = dot(query, key, 1, 1)
        weights = jnp.where(allowed, scores, 0.0).astype(BF16)
        gv_ref[:, head(h)] = dot(weights, pre, 0, 0)
        grad_scores = dot(pre, value, 1, 1)
        grad_weights = jnp.where(allowed, grad_scores, 0.0).astype(BF16)
        gk_ref[:, head(h)] = dot(grad_weights, query, 0, 0)
        carried = state_ref[h * DH : (h + 1) * DH, :].astype(BF16)
        head_pre = jnp.where(opened, pre, jnp.zeros((), BF16))
        gq_ref[:, head(h)] = (
            dot(grad_weights, key, 1, 0) + dot(head_pre, carried, 1, 1)
        ).astype(BF16)


def final_kernel(off_ref, k_ref, v_ref, recv_ref, gk_ref, gv_ref, outk_ref, outv_ref, gain_ref):
    length, width = k_ref.shape
    _, last, _ = bounds(off_ref)
    tail = row_mask(length, last=last)
    for h in range(width // DH):
        rows = [9 * (h * (DH // 8) + j) for j in range(DH // 8)]
        later = jnp.concatenate([recv_ref[r : r + 8, :] for r in rows], axis=0).astype(BF16)
        keys = jnp.where(tail, k_ref[:, head(h)], jnp.zeros((), BF16))
        values = jnp.where(tail, v_ref[:, head(h)], jnp.zeros((), BF16))
        outk_ref[:, head(h)] = (gk_ref[:, head(h)] + dot(values, later, 1, 1)).astype(BF16)
        outv_ref[:, head(h)] = (gv_ref[:, head(h)] + dot(keys, later, 1, 0)).astype(BF16)
        gain_ref[h : h + 1, :] = recv_ref[9 * h + 8 : 9 * h + 9, :]


def call(kernel, outs, flops, bytes_accessed, *args):
    return pl.pallas_call(
        kernel,
        out_shape=[jax.ShapeDtypeStruct(s, d) for s, d in outs],
        in_specs=[SMEM if a.dtype == jnp.int32 else VMEM for a in args],
        out_specs=[VMEM] * len(outs),
        cost_estimate=pl.CostEstimate(
            flops=flops, bytes_accessed=bytes_accessed, transcendentals=0
        ),
    )(*args)


def exchanged(rows, per):
    count = rows.shape[0] // per
    shape = (count, per, DH) if per == 8 else (count, per, 1, DH)
    return lax.all_to_all(rows.reshape(shape), "seq", 0, 0).reshape(rows.shape)


def shards(query, key_rows, value, gain, grad_out, start_offset):
    q, k, v, g = query[0], key_rows[0], value[0], grad_out[0]
    length, width = q.shape
    off = start_offset
    gain = gain.reshape(1, width)
    count = lax.axis_size("seq")
    wide = (length, width)
    mega = 1 << 20
    (tails,) = call(tail_kernel, [((count * 9, DH), F32)], 34 * mega, mega, off, k, v)
    tails = exchanged(tails, 9)
    (local,) = call(local_kernel, [(wide, F32)], 134 * mega, mega, off, q, k, v)
    (prefixes,) = call(prefix_kernel, [((count * 8, DH), F32)], mega, mega, tails)
    state = exchanged(prefixes, 8)
    att, sums = call(
        attend_kernel, [(wide, F32), ((16, DH), F32)], 34 * mega, mega, off, q, local, state, g, gain
    )
    sums = lax.all_to_all(sums.reshape(4, 4, DH), "tensor", 0, 0).reshape(16, DH)
    out, pre, grad_states = call(
        norm_kernel,
        [(wide, BF16), (wide, BF16), ((count * 9, DH), F32)],
        34 * mega,
        mega,
        off,
        q,
        att,
        g,
        gain,
        sums,
    )
    grad_states = exchanged(grad_states, 9)
    gq, gk, gv = call(
        grads_kernel,
        [(wide, BF16), (wide, F32), (wide, F32)],
        340 * mega,
        3 * mega,
        off,
        q,
        k,
        v,
        pre,
        state,
    )
    (suffixes,) = call(suffix_kernel, [((count * 9, DH), F32)], mega, mega, tails, grad_states)
    later = exchanged(suffixes, 9)
    gk, gv, gain_sum = call(
        final_kernel,
        [(wide, BF16), (wide, BF16), ((width // DH, DH), F32)],
        68 * mega,
        2 * mega,
        off,
        k,
        v,
        later,
        gk,
        gv,
    )
    grad_gain = lax.psum(gain_sum, "dp").reshape(width)
    return out[None], gq[None], gk[None], gv[None], grad_gain


def solution(mesh):
    wide = P("dp", "seq", "tensor")
    return jax.shard_map(
        shards,
        mesh=mesh,
        in_specs=(wide, wide, wide, P("tensor"), wide, P("dp", "seq")),
        out_specs=(wide, wide, wide, wide, P("tensor")),
        check_vma=False,
    )
```

time: 743 us -> 119 us (0.16)
  the two profiles are of different devices: /device:TPU:2 before, /device:TPU:1 now
where the time goes in v1:
time: 119 us; the launch traced here: 118 us
  blocking collectives  66.6 us (56%)
  Pallas kernels  19.5 us (16%)
  waiting for transfers between devices  18.8 us (16%)
  starting transfers between devices  10.6 us (9%)
  local copies, waits for them, and re-layouts  2.1 us (2%)
    all_to_all x2, blocking collectives, exchanged(): return lax.all_to_all(rows.reshape(shape), 'seq', 0, 0).reshape(rows.shape)  48.9 us
    pallas_call x8, Pallas kernels, call(): pl.pallas_call(kernel, out_shape=[jax.ShapeDtypeStruct(s, d) for s, d in...  19.5 us
    all_to_all x2, waiting for transfers between devices, exchanged(): return lax.all_to_all(rows.reshape(shape), 'seq', 0, 0).reshape(rows.shape)  18.8 us
    all_to_all x2, starting transfers between devices, exchanged(): return lax.all_to_all(rows.reshape(shape), 'seq', 0, 0).reshape(rows.shape)  10.6 us
    psum x1, blocking collectives, shards(): grad_gain = lax.psum(gain_sum, 'dp').reshape(width)  9.41 us
    all_to_all x1, blocking collectives, shards(): lax.all_to_all(sums.reshape(4, 4, DH), 'tensor', 0, 0).reshape(16, DH)  8.29 us
  transfers between devices with their start and end apart: 2, of which 2 were waited for; matrix products, arithmetic and copies ran while one was open for 0% of the time, Pallas kernels for 5%

profile of v1, /device:TPU:1, one launch (start us, length us, event | category | flops | bytes accessed | tf_op | source)
XLA Modules:
  0.0 118.2 jit_solution(2223931685984507311)
XLA Ops:
  0.6 2.1 %shard_map.102 = f32[576,128]{1,0:T(8,128)} custom-call(s32[1,4]{1,0:T(1,128)} %off_ref.11, bf16[256,512]{1,0:T(8,128)(2,1)} %bitcast.26, bf16[256,512]{1,0:T(8,128)(2,1)} %bitcast.30), custom_call_target="tpu_custom_call" | custom-call | flops 35651584 | bytes 1048576 | tf_op jit(solution)/shard_map/pallas_call | solution.py:193
  2.7 30.5 %all_to_all.25 = f32[64,9,1,128]{3,2,1,0:T(1,128)} all-to-all(f32[64,9,1,128]{3,2,1,0:T(1,128)} %bitcast.37), channel_id=1, replica_groups=mesh['dp'=2,'seq'=64,'tensor'=4] {'seq'}, dimensions={0} | all-to-all | bytes 589824 | tf_op jit(solution)/shard_map/all_to_all | solution.py:207
  33.2 1.8 %shard_map.103 = f32[512,128]{1,0:T(8,128)} custom-call(f32[576,128]{1,0:T(8,128)} %bitcast.20), custom_call_target="tpu_custom_call" | custom-call | flops 1048576 | bytes 1048576 | tf_op jit(solution)/shard_map/pallas_call | solution.py:193
  35.0 5.9 %all-to-all-start.1 = ((f32[64,8,128]{2,1,0:T(8,128)}), f32[64,8,128]{2,1,0:T(8,128)S(1)}, u32[]{:S(2)}, u32[]{:S(2)}) async-start(f32[64,8,128]{2,1,0:T(8,128)} %bitcast.42), calls=%async_computation.1 | async-start | bytes 524288 | tf_op jit(solution)/shard_map/all_to_all | solution.py:207
  40.9 2.6 %shard_map.101.local_ref = f32[256,512]{1,0:T(8,128)} custom-call(s32[1,4]{1,0:T(1,128)} %off_ref.11, bf16[256,512]{1,0:T(8,128)(2,1)} %bitcast.22, bf16[256,512]{1,0:T(8,128)(2,1)} %bitcast.27, bf16[256,512]{1,0:T(8,128)(2,1)} %bitcast.31), custom_call_target="tpu_custom_call" | custom-call | flops 140509184 | bytes 1048576 | tf_op jit(solution)/shard_map/pallas_call | solution.py:193
  43.5 9.9 %all-to-all-done.1 = f32[64,8,128]{2,1,0:T(8,128)S(1)} async-done(((f32[64,8,128]{2,1,0:T(8,128)}), f32[64,8,128]{2,1,0:T(8,128)S(1)}, u32[]{:S(2)}, u32[]{:S(2)}) %all-to-all-start.1) | async-done | bytes 262176 | tf_op jit(solution)/shard_map/all_to_all | solution.py:207
  53.4 0.0 copy-start.1
  53.4 0.7 copy-done.1
  54.1 2.3 %shard_map.104 = (f32[256,512]{1,0:T(8,128)}, f32[16,128]{1,0:T(8,128)}) custom-call(s32[1,4]{1,0:T(1,128)} %off_ref.11, bf16[256,512]{1,0:T(8,128)(2,1)} %bitcast.23, f32[256,512]{1,0:T(8,128)} %shard_map.101.local_ref, f32[512,128]{1,0:T(8,128)} %bitcast.38, bf16[256,512]{1,0:T(8,128)(2,1)} %bitcast.40, f32[1,512]{1,0:T(1,128)} %bitcast.45), custom_call_target="tpu_custom_call" | custom-call | flops 35651584 | bytes 1048576 | tf_op jit(solution)/shard_map/pallas_call | solution.py:193
  56.4 8.3 %all_to_all.26 = f32[4,4,128]{2,1,0:T(4,128)} all-to-all(f32[4,4,128]{2,1,0:T(4,128)} %bitcast.47), channel_id=1, replica_groups=mesh['dp'=2,'seq'=64,'tensor'=4] {'tensor'}, dimensions={0} | all-to-all | bytes 16384 | tf_op jit(solution)/shard_map/all_to_all | solution.py:226
  64.7 2.4 %shard_map.105 = (bf16[256,512]{1,0:T(8,128)(2,1)}, bf16[256,512]{1,0:T(8,128)(2,1)}, f32[576,128]{1,0:T(8,128)}) custom-call(s32[1,4]{1,0:T(1,128)} %off_ref.11, bf16[256,512]{1,0:T(8,128)(2,1)} %bitcast.24, f32[256,512]{1,0:T(8,128)} %get-tuple-element.16.att_ref, bf16[256,512]{1,0:T(8,128)(2,1)} %bitcast.41, f32[1,512]{1,0:T(1,128)} %bitcast.46, ...), custom_call_target="tpu_custom_call" | custom-call | flops 35651584 | bytes 1048576 | tf_op jit(solution)/shard_map/pallas_call | solution.py:193
  67.1 18.4 %all_to_all.27 = f32[64,9,1,128]{3,2,1,0:T(1,128)} all-to-all(f32[64,9,1,128]{3,2,1,0:T(1,128)} %bitcast.43), channel_id=1, replica_groups=mesh['dp'=2,'seq'=64,'tensor'=4] {'seq'}, dimensions={0} | all-to-all | bytes 589824 | tf_op jit(solution)/shard_map/all_to_all | solution.py:207
  85.6 1.9 %shard_map.107 = f32[576,128]{1,0:T(8,128)} custom-call(f32[576,128]{1,0:T(8,128)} %bitcast.21, f32[576,128]{1,0:T(8,128)} %bitcast.35), custom_call_target="tpu_custom_call" | custom-call | flops 1048576 | bytes 1048576 | tf_op jit(solution)/shard_map/pallas_call | solution.py:193
  87.5 4.6 %all-to-all-start.4 = ((f32[64,9,1,128]{3,2,1,0:T(1,128)}), f32[64,9,1,128]{3,2,1,0:T(1,128)S(1)}, u32[]{:S(2)}, u32[]{:S(2)}) async-start(f32[64,9,1,128]{3,2,1,0:T(1,128)} %bitcast.34), calls=%async_computation.4 | async-start | bytes 589824 | tf_op jit(solution)/shard_map/all_to_all | solution.py:207
  92.1 3.9 %shard_map.106 = (bf16[256,512]{1,0:T(8,128)(2,1)}, f32[256,512]{1,0:T(8,128)}, f32[256,512]{1,0:T(8,128)}) custom-call(s32[1,4]{1,0:T(1,128)} %off_ref.11, bf16[256,512]{1,0:T(8,128)(2,1)} %bitcast.25, bf16[256,512]{1,0:T(8,128)(2,1)} %bitcast.28, bf16[256,512]{1,0:T(8,128)(2,1)} %bitcast.32, bf16[256,512]{1,0:T(8,128)(2,1)} %get-tuple-element.19.pre_ref, ...), custom_call_target="tpu_custom_call" | custom-call | flops 356515840 | bytes 3145728 | tf_op jit(solution)/shard_map/pallas_call | solution.py:193
  96.0 8.9 %all-to-all-done.4 = f32[64,9,1,128]{3,2,1,0:T(1,128)S(1)} async-done(((f32[64,9,1,128]{3,2,1,0:T(1,128)}), f32[64,9,1,128]{3,2,1,0:T(1,128)S(1)}, u32[]{:S(2)}, u32[]{:S(2)}) %all-to-all-start.4) | async-done | bytes 294944 | tf_op jit(solution)/shard_map/all_to_all | solution.py:207
  104.9 0.0 copy-start
  104.9 0.7 copy-done
  105.6 2.5 %shard_map.108 = (bf16[256,512]{1,0:T(8,128)(2,1)}, bf16[256,512]{1,0:T(8,128)(2,1)}, f32[4,128]{1,0:T(4,128)}) custom-call(s32[1,4]{1,0:T(1,128)} %off_ref.11, bf16[256,512]{1,0:T(8,128)(2,1)} %bitcast.29, bf16[256,512]{1,0:T(8,128)(2,1)} %bitcast.33, f32[576,128]{1,0:T(8,128)} %bitcast.36, f32[256,512]{1,0:T(8,128)} %get-tuple-element.22.gk_ref, ...), custom_call_target="tpu_custom_call" | custom-call | flops 71303168 | bytes 2097152 | tf_op jit(solution)/shard_map/pallas_call | solution.py:193
  108.1 0.0 copy-start.2
  108.1 0.7 copy-done.2
  108.8 9.4 %psum.7 = f32[512]{0:T(512)} all-reduce(f32[512]{0:T(512)S(1)} %bitcast.48), channel_id=1, replica_groups=mesh['dp'=2,'seq'=64,'tensor'=4] {'dp'}, use_global_device_ids=true, to_apply=%region_0.0 | all-reduce | flops 512 | bytes 4096 | tf_op jit(solution)/shard_map/psum | solution.py:266
Async XLA Ops:
  35.0 18.4 %all-to-all-start.1 = ((f32[64,8,128]{2,1,0:T(8,128)}), f32[64,8,128]{2,1,0:T(8,128)S(1)}, u32[]{:S(2)}, u32[]{:S(2)}) async-start(f32[64,8,128]{2,1,0:T(8,128)} %bitcast.42), calls=%async_computation.1 | async-start | bytes 524288 | tf_op jit(solution)/shard_map/all_to_all | solution.py:207
  53.4 0.7 copy-start.1
  87.5 17.4 %all-to-all-start.4 = ((f32[64,9,1,128]{3,2,1,0:T(1,128)}), f32[64,9,1,128]{3,2,1,0:T(1,128)S(1)}, u32[]{:S(2)}, u32[]{:S(2)}) async-start(f32[64,9,1,128]{3,2,1,0:T(1,128)} %bitcast.34), calls=%async_computation.4 | async-start | bytes 589824 | tf_op jit(solution)/shard_map/all_to_all | solution.py:207
  104.9 0.7 copy-start
  108.1 0.7 copy-start.2

commit v2 on v1

v2 whole, which is shorter than its diff:
```python
import jax
import jax.numpy as jnp
from jax import lax
from jax.experimental import pallas as pl
from jax.experimental.pallas import tpu as pltpu
from jax.sharding import PartitionSpec as P

DH = 128
BLK = 64
CH = 2048
EPS = 1e-05
ROOT = 36
VMEM = pl.BlockSpec(memory_space=pltpu.VMEM)
SMEM = pl.BlockSpec(memory_space=pltpu.SMEM)
HBM = pl.BlockSpec(memory_space=pltpu.HBM)
F32 = jnp.float32
BF16 = jnp.bfloat16


def dot(a, b, ca, cb):
    return lax.dot_general(a, b, (((ca,), (cb,)), ((), ())), preferred_element_type=F32)


def bounds(off_ref):
    first, last, count = jnp.int32(1 << 20), jnp.int32(-1), jnp.int32(0)
    for b in range(off_ref.shape[1]):
        off = off_ref[0, b]
        present = off < BLK
        first = jnp.minimum(first, jnp.where(present, b * BLK + off, 1 << 20))
        last = jnp.maximum(last, jnp.where(present, b * BLK + off, -1))
        count += present.astype(jnp.int32)
    return first, last, count


def labels_of(off_ref, pos):
    labels = jnp.zeros(pos.shape, jnp.int32)
    for b in range(off_ref.shape[1]):
        off = off_ref[0, b]
        start = jnp.where(off < BLK, b * BLK + off, 1 << 20)
        labels += (pos >= start).astype(jnp.int32)
    return labels


def allowed_of(off_ref, length):
    t = lax.broadcasted_iota(jnp.int32, (length, length), 0)
    s = lax.broadcasted_iota(jnp.int32, (length, length), 1)
    rows = labels_of(off_ref, lax.broadcasted_iota(jnp.int32, (length, 1), 0))
    cols = labels_of(off_ref, lax.broadcasted_iota(jnp.int32, (1, length), 1))
    return (rows == cols) & (s <= t)


def row_mask(length, first=None, last=None):
    pos = lax.broadcasted_iota(jnp.int32, (length, DH), 0)
    return pos < first if last is None else pos >= last


def put_slices(send_ref, h, state):
    for j in range(DH // 8):
        at = 9 * (h * (DH // 8) + j)
        send_ref[at : at + 8, :] = state[8 * j : 8 * j + 8, :]


def head(h):
    return slice(h * DH, (h + 1) * DH)


def tail_kernel(off_hbm, k_hbm, v_hbm, send_hbm, off_ref, k_ref, v_ref, send_ref, sems, sent):
    copies = [
        pltpu.make_async_copy(source, target, sems.at[i])
        for i, (source, target) in enumerate(
            ((off_hbm, off_ref), (k_hbm, k_ref), (v_hbm, v_ref))
        )
    ]
    for copy in copies:
        copy.start()
    length, width = k_ref.shape
    copies[0].wait()
    _, last, count = bounds(off_ref)
    tail = row_mask(length, last=last)
    keep = jnp.full((1, DH), jnp.where(count > 0, 0.0, 1.0), F32)
    for j in range(send_ref.shape[0] // 9):
        send_ref[9 * j + 8 : 9 * j + 9, :] = keep
    copies[1].wait()
    copies[2].wait()
    outs = []
    for h in range(width // DH):
        keys = jnp.where(tail, k_ref[:, head(h)], jnp.zeros((), BF16))
        put_slices(send_ref, h, dot(keys, v_ref[:, head(h)], 0, 0))
        rows = slice(h * 9 * (DH // 8), (h + 1) * 9 * (DH // 8))
        outs.append(pltpu.make_async_copy(send_ref.at[rows], send_hbm.at[rows], sent.at[h]))
        outs[-1].start()
    for copy in outs:
        copy.wait()


def local_kernel(off_ref, q_ref, k_ref, v_ref, g_ref, gain_ref, out_ref, scaled_ref, token_ref):
    length, width = q_ref.shape
    allowed = allowed_of(off_ref, length)
    for h in range(width // DH):
        scores = dot(q_ref[:, head(h)], k_ref[:, head(h)], 1, 1)
        weights = jnp.where(allowed, scores, 0.0).astype(BF16)
        out_ref[:, head(h)] = dot(weights, v_ref[:, head(h)], 1, 0)
        scaled_ref[:, head(h)] = gain_ref[:, head(h)] * g_ref[:, head(h)].astype(F32)
    token_ref[...] = jnp.zeros_like(token_ref)


def order_of(count):
    side = 8

    def distance(w):
        steps = (abs(w // side - ROOT // side), abs(w % side - ROOT % side))
        return sum(min(d, side - d) for d in steps)

    return [ROOT] + sorted((w for w in range(count) if w != ROOT), key=lambda w: -distance(w))


def slots_of(count):
    order = order_of(count)
    return [order.index(w) for w in range(count)]


def prefix_kernel(recv_ref, token_ref, send_ref):
    carry = token_ref[...]
    for w in slots_of(recv_ref.shape[0] // 9):
        send_ref[8 * w : 8 * w + 8, :] = carry
        keep = jnp.broadcast_to(recv_ref[9 * w + 8 : 9 * w + 9, :], (8, DH))
        carry = recv_ref[9 * w : 9 * w + 8, :] + carry * keep


def attend_kernel(off_ref, q_ref, local_ref, state_ref, scaled_ref, att_ref, sums_ref):
    length, width = q_ref.shape
    first, _, _ = bounds(off_ref)
    opened = row_mask(length, first=first)
    squares = jnp.zeros((length, DH), F32)
    products = jnp.zeros((length, DH), F32)
    for h in range(width // DH):
        carried = state_ref[h * DH : (h + 1) * DH, :].astype(BF16)
        carried_out = dot(q_ref[:, head(h)], carried, 1, 0)
        att = local_ref[:, head(h)] + jnp.where(opened, carried_out, 0.0)
        att_ref[:, head(h)] = att
        squares += att * att
        products += scaled_ref[:, head(h)] * att
    row = 0
    for total in (squares, products):
        for half in range(length // DH):
            line = jnp.sum(total[half * DH : (half + 1) * DH, :].T, axis=0, keepdims=True)
            for c in range(4):
                sums_ref[4 * c + row : 4 * c + row + 1, :] = line
            row += 1


def columns_of(sums_ref, length):
    total = sums_ref[0:4, :] + sums_ref[4:8, :] + sums_ref[8:12, :] + sums_ref[12:16, :]
    halves = length // DH
    inv = lax.rsqrt(total[0:halves, :] / CH + EPS)
    mean = inv * total[halves : 2 * halves, :] / CH
    cols = jnp.concatenate([inv, mean, inv, mean], axis=0).T
    inverse = jnp.concatenate([cols[:, i : i + 1] for i in range(halves)], axis=0)
    mean = jnp.concatenate([cols[:, halves + i : halves + i + 1] for i in range(halves)], axis=0)
    return jnp.broadcast_to(inverse, (length, DH)), jnp.broadcast_to(mean, (length, DH))


def pre_kernel(
    off_ref, q_ref, att_ref, g_ref, scaled_ref, gain_ref, sums_ref,
    pre_ref, out_hbm, send_hbm, out_ref, send_ref, sems,
):
    length, width = q_ref.shape
    first, _, _ = bounds(off_ref)
    opened = row_mask(length, first=first)
    inverse, mean = columns_of(sums_ref, length)
    copies, parts, pres = [], [], []
    for h in range(width // DH):
        normed = att_ref[:, head(h)] * inverse
        out_ref[:, head(h)] = (gain_ref[:, head(h)] * normed).astype(BF16)
        copies.append(
            pltpu.make_async_copy(
                out_ref.at[:, head(h)], out_hbm.at[:, head(h)], sems.at[0, h]
            )
        )
        copies[-1].start()
        pre = inverse * (scaled_ref[:, head(h)] - normed * mean)
        pre_ref[:, head(h)] = pre.astype(BF16)
        pres.append(jnp.where(opened, pre, 0.0).astype(BF16))
        upstream = g_ref[:, head(h)].astype(F32)
        parts.append(jnp.sum(upstream * normed, axis=0, keepdims=True))
    part = jnp.concatenate(parts, axis=0)
    for j in range(send_ref.shape[0] // 12):
        send_ref[12 * j + 8 : 12 * j + 12, :] = part
    for h in range(width // DH):
        state = dot(q_ref[:, head(h)], pres[h], 0, 0)
        for j in range(DH // 8):
            at = 12 * (h * (DH // 8) + j)
            send_ref[at : at + 8, :] = state[8 * j : 8 * j + 8, :]
        rows = slice(h * 12 * (DH // 8), (h + 1) * 12 * (DH // 8))
        copies.append(pltpu.make_async_copy(send_ref.at[rows], send_hbm.at[rows], sems.at[1, h]))
        copies[-1].start()
    for copy in copies:
        copy.wait()


def suffix_kernel(flags_ref, recv_ref, token_ref, send_ref, after_ref):
    carry = token_ref[...]
    after_ref[...] = carry
    for w in reversed(slots_of(recv_ref.shape[0] // 12)):
        send_ref[8 * w : 8 * w + 8, :] = carry
        keep = jnp.broadcast_to(flags_ref[9 * w + 8 : 9 * w + 9, :], (8, DH))
        carry = recv_ref[12 * w : 12 * w + 8, :] + carry * keep


def part_kernel(recv_ref, token_ref, part_ref):
    sums = [token_ref[4 * (i % 2) : 4 * (i % 2) + 4, :] for i in range(4)]
    for w in range(recv_ref.shape[0] // 12):
        sums[w % 4] += recv_ref[12 * w + 8 : 12 * w + 12, :]
    part_ref[...] = (sums[0] + sums[1]) + (sums[2] + sums[3])


def grads_kernel(
    off_ref, q_ref, k_ref, v_ref, pre_ref, state_ref, gq_ref, gk_ref, gv_ref, token_ref
):
    length, width = q_ref.shape
    token_ref[...] = jnp.zeros_like(token_ref)
    first, _, _ = bounds(off_ref)
    opened = row_mask(length, first=first)
    allowed = allowed_of(off_ref, length)
    for h in range(width // DH):
        query, key, value, pre = (r[:, head(h)] for r in (q_ref, k_ref, v_ref, pre_ref))
        scores = dot(query, key, 1, 1)
        weights = jnp.where(allowed, scores, 0.0).astype(BF16)
        gv_ref[:, head(h)] = dot(weights, pre, 0, 0)
        grad_scores = dot(pre, value, 1, 1)
        grad_weights = jnp.where(allowed, grad_scores, 0.0).astype(BF16)
        gk_ref[:, head(h)] = dot(grad_weights, query, 0, 0)
        carried = state_ref[h * DH : (h + 1) * DH, :].astype(BF16)
        carried_grad = jnp.where(opened, dot(pre, carried, 1, 1), 0.0)
        gq_ref[:, head(h)] = (dot(grad_weights, key, 1, 0) + carried_grad).astype(BF16)


def final_kernel(
    off_ref, k_ref, v_ref, later_ref, gk_ref, gv_ref, part_ref, other_ref,
    outk_hbm, outv_hbm, gain_ref, outk, outv, sems,
):
    length, width = k_ref.shape
    _, last, _ = bounds(off_ref)
    tail = row_mask(length, last=last)
    copies = []
    for h in range(width // DH):
        later = later_ref[h * DH : (h + 1) * DH, :].astype(BF16)
        from_values = jnp.where(tail, dot(v_ref[:, head(h)], later, 1, 1), 0.0)
        from_keys = jnp.where(tail, dot(k_ref[:, head(h)], later, 1, 0), 0.0)
        outk[:, head(h)] = (gk_ref[:, head(h)] + from_values).astype(BF16)
        outv[:, head(h)] = (gv_ref[:, head(h)] + from_keys).astype(BF16)
        for i, (source, target) in enumerate(((outk, outk_hbm), (outv, outv_hbm))):
            copies.append(
                pltpu.make_async_copy(
                    source.at[:, head(h)], target.at[:, head(h)], sems.at[i, h]
                )
            )
            copies[-1].start()
    gain_ref[...] = part_ref[...] + other_ref[...]
    for copy in copies:
        copy.wait()


def call(kernel, outs, flops, bytes_accessed, *args, ins=None, out_specs=None, scratch=(), grant=12):
    return pl.pallas_call(
        kernel,
        out_shape=[jax.ShapeDtypeStruct(s, d) for s, d in outs],
        in_specs=ins or [SMEM if a.dtype == jnp.int32 else VMEM for a in args],
        out_specs=out_specs or [VMEM] * len(outs),
        scratch_shapes=list(scratch),
        compiler_params=pltpu.CompilerParams(vmem_limit_bytes=grant << 20),
        cost_estimate=pl.CostEstimate(
            flops=flops, bytes_accessed=bytes_accessed, transcendentals=0
        ),
    )(*args)


def exchanged(rows, per):
    count = rows.shape[0] // per
    tile = {8: (8,), 9: (9, 1), 12: (3, 4)}[per]
    groups = [order_of(count)]
    moved = lax.all_to_all(
        rows.reshape((count, *tile, DH)), "seq", 0, 0, axis_index_groups=groups
    )
    return moved.reshape(rows.shape)


def shards(query, key_rows, value, gain, grad_out, start_offset):
    q, k, v, g = query[0], key_rows[0], value[0], grad_out[0]
    length, width = q.shape
    heads = width // DH
    off = start_offset
    gain = gain.reshape(1, width)
    count = lax.axis_size("seq")
    wide = (length, width)
    mega = 1 << 20
    dma = pltpu.SemaphoreType.DMA
    (tails,) = call(
        tail_kernel,
        [((count * 9, DH), F32)],
        34 * mega,
        mega,
        off,
        k,
        v,
        ins=[HBM] * 3,
        out_specs=[HBM],
        scratch=(
            pltpu.SMEM(off.shape, jnp.int32),
            pltpu.VMEM(wide, BF16),
            pltpu.VMEM(wide, BF16),
            pltpu.VMEM((count * 9, DH), F32),
            dma((3,)),
            dma((heads,)),
        ),
        grant=63,
    )
    tails = exchanged(tails, 9)
    token = (8, DH)
    local, scaled, ready = call(
        local_kernel,
        [(wide, F32), (wide, F32), (token, F32)],
        134 * mega,
        mega,
        off,
        q,
        k,
        v,
        g,
        gain,
    )
    (prefixes,) = call(prefix_kernel, [((count * 8, DH), F32)], mega, mega, tails, ready)
    state = exchanged(prefixes, 8)
    att, sums = call(
        attend_kernel, [(wide, F32), ((16, DH), F32)], 34 * mega, mega, off, q, local, state, scaled
    )
    sums = lax.all_to_all(
        sums.reshape(4, 4, DH), "tensor", 0, 0, axis_index_groups=[[2, 3, 1, 0]]
    ).reshape(16, DH)
    pre, out, grad_states = call(
        pre_kernel,
        [(wide, BF16), (wide, BF16), ((count * 12, DH), F32)],
        34 * mega,
        mega,
        off,
        q,
        att,
        g,
        scaled,
        gain,
        sums,
        out_specs=[VMEM, HBM, HBM],
        scratch=(
            pltpu.VMEM(wide, BF16),
            pltpu.VMEM((count * 12, DH), F32),
            dma((2, heads)),
        ),
    )
    grad_states = exchanged(grad_states, 12)
    gq, gk, gv, ready = call(
        grads_kernel,
        [(wide, BF16), (wide, F32), (wide, F32), (token, F32)],
        340 * mega,
        3 * mega,
        off,
        q,
        k,
        v,
        pre,
        state,
    )
    suffixes, ready = call(
        suffix_kernel,
        [((count * 8, DH), F32), (token, F32)],
        mega,
        mega,
        tails,
        grad_states,
        ready,
    )
    later = exchanged(suffixes, 8)
    (part,) = call(part_kernel, [((heads, DH), F32)], mega, mega, grad_states, ready)
    other = lax.ppermute(part, "dp", [(0, 1), (1, 0)])
    gk, gv, gain_sum = call(
        final_kernel,
        [(wide, BF16), (wide, BF16), ((heads, DH), F32)],
        68 * mega,
        2 * mega,
        off,
        k,
        v,
        later,
        gk,
        gv,
        part,
        other,
        out_specs=[HBM, HBM, VMEM],
        scratch=(pltpu.VMEM(wide, BF16), pltpu.VMEM(wide, BF16), dma((2, heads))),
    )
    return out[None], gq[None], gk[None], gv[None], gain_sum.reshape(width)


def solution(mesh):
    wide = P("dp", "seq", "tensor")
    return jax.shard_map(
        shards,
        mesh=mesh,
        in_specs=(wide, wide, wide, P("tensor"), wide, P("dp", "seq")),
        out_specs=(wide, wide, wide, wide, P("tensor")),
        check_vma=False,
    )
```

time: 119 us -> 100 us (0.84)
  the two profiles are of different devices: /device:TPU:1 before, /device:TPU:2 now
where the time goes in v2:
time: 100 us; the launch traced here: 99.8 us
  starting transfers between devices  47.3 us (47%)
  blocking collectives  26.2 us (26%)
  waiting for transfers between devices  12.1 us (12%)
  Pallas kernels  12 us (12%)
  local copies, waits for them, and re-layouts  1.44 us (1%)
    all_to_all x3, starting transfers between devices, exchanged(): lax.all_to_all(rows.reshape((count, *tile, DH)), 'seq', 0, 0, axis_index_...  45.4 us
    all_to_all x1, blocking collectives, exchanged(): lax.all_to_all(rows.reshape((count, *tile, DH)), 'seq', 0, 0, axis_index_...  18.5 us
    pallas_call x9, Pallas kernels, call(): pl.pallas_call(kernel, out_shape=[jax.ShapeDtypeStruct(s, d) for s, d in...  12 us
    all_to_all x3, waiting for transfers between devices, exchanged(): lax.all_to_all(rows.reshape((count, *tile, DH)), 'seq', 0, 0, axis_index_...  11 us
    all_to_all x1, blocking collectives, shards(): lax.all_to_all(sums.reshape(4, 4, DH), 'tensor', 0, 0, axis_index_groups=...  7.69 us
  transfers between devices with their start and end apart: 4, of which 4 were waited for; matrix products, arithmetic and copies ran while one was open for 0% of the time, Pallas kernels for 4%

profile of v2, /device:TPU:2, one launch (start us, length us, event | category | flops | bytes accessed | tf_op | source)
XLA Modules:
  0.0 99.8 jit_solution(1190233688019086590)
XLA Ops:
  0.7 2.1 %shard_map.102 = f32[576,128]{1,0:T(8,128)} custom-call(s32[1,4]{1,0:T(1,128)} %off_ref.9, bf16[256,512]{1,0:T(8,128)(2,1)} %bitcast.28, bf16[256,512]{1,0:T(8,128)(2,1)} %bitcast.32), custom_call_target="tpu_custom_call" | custom-call | flops 35651584 | bytes 1048576 | tf_op jit(solution)/shard_map/pallas_call | solution.py:265
  2.7 0.0 copy-start
  2.7 0.0 copy-start.1
  2.8 19.9 %all-to-all-start = ((f32[64,9,1,128]{3,2,1,0:T(1,128)}), f32[64,9,1,128]{3,2,1,0:T(1,128)S(1)}, u32[]{:S(2)}, u32[]{:S(2)}) async-start(f32[64,9,1,128]{3,2,1,0:T(1,128)} %bitcast.46), calls=%async_computation | async-start | bytes 589824 | tf_op jit(solution)/shard_map/all_to_all | solution.py:282
  22.6 0.0 copy-start.7
  22.7 0.0 copy-start.6
  22.7 0.6 copy-done.7
  23.3 1.2 %shard_map.101 = (f32[256,512]{1,0:T(8,128)S(1)}, f32[256,512]{1,0:T(8,128)S(1)}, f32[8,128]{1,0:T(8,128)S(1)}) custom-call(s32[1,4]{1,0:T(1,128)S(1)} %copy-done.6, bf16[256,512]{1,0:T(8,128)(2,1)S(1)} %bitcast.24, bf16[256,512]{1,0:T(8,128)(2,1)S(1)} %bitcast.29, bf16[256,512]{1,0:T(8,128)(2,1)S(1)} %bitcast.33, bf16[256,512]{1,0:T(8,128)(2,1)S(1)} %bitcast.40, ...), custom_call_target="tpu_custom_call" | custom-call | flops 140509184 | bytes 1048576 | tf_op jit(solution)/shard_map/pallas_call | solution.py:265
  24.5 0.8 copy-done.4
  25.3 4.3 %all-to-all-done = f32[64,9,1,128]{3,2,1,0:T(1,128)S(1)} async-done(((f32[64,9,1,128]{3,2,1,0:T(1,128)}), f32[64,9,1,128]{3,2,1,0:T(1,128)S(1)}, u32[]{:S(2)}, u32[]{:S(2)}) %all-to-all-start) | async-done | bytes 294944 | tf_op jit(solution)/shard_map/all_to_all | solution.py:282
  29.6 0.1 shard_map.103
  29.7 18.5 %all_to_all.25 = f32[64,8,128]{2,1,0:T(8,128)S(1)} all-to-all(f32[64,8,128]{2,1,0:T(8,128)S(1)} %bitcast.36), channel_id=1, replica_groups={{144,0,4,28,32,224,8,24,36,60,64,192,228,252,12,20,40,56,68,92,96,160,1..., dimensions={0} | all-to-all | bytes 524288 | tf_op jit(solution)/shard_map/all_to_all | solution.py:282
  48.3 0.9 shard_map.104
  49.2 7.7 %all_to_all.26 = f32[4,4,128]{2,1,0:T(4,128)S(1)} all-to-all(f32[4,4,128]{2,1,0:T(4,128)S(1)} %bitcast.45), channel_id=1, replica_groups={{2,3,1,0},{6,7,5,4},{10,11,9,8},{14,15,13,12},{18,19,17,16},{22,23,21,2..., dimensions={0} | all-to-all | bytes 16384 | tf_op jit(solution)/shard_map/all_to_all | solution.py:337
  56.9 1.9 %shard_map.105 = (bf16[256,512]{1,0:T(8,128)(2,1)S(1)}, bf16[256,512]{1,0:T(8,128)(2,1)}, f32[768,128]{1,0:T(8,128)}) custom-call(s32[1,4]{1,0:T(1,128)S(1)} %copy-done.6, bf16[256,512]{1,0:T(8,128)(2,1)S(1)} %bitcast.26, f32[256,512]{1,0:T(8,128)S(1)} %get-tuple-element.25.att_ref, bf16[256,512]{1,0:T(8,128)(2,1)S(1)} %bitcast.41, ...), custom_call_target="tpu_custom_call" | custom-call | flops 35651584 | bytes 1048576 | tf_op jit(solution)/shard_map/pallas_call | solution.py:265
  58.7 12.6 %all-to-all-start.3 = ((f32[64,3,4,128]{3,2,1,0:T(4,128)}), f32[64,3,4,128]{3,2,1,0:T(4,128)S(1)}, u32[]{:S(2)}, u32[]{:S(2)}) async-start(f32[64,3,4,128]{3,2,1,0:T(4,128)} %bitcast.13), calls=%async_computation.3 | async-start | bytes 786432 | tf_op jit(solution)/shard_map/all_to_all | solution.py:282
  71.4 2.8 %shard_map.106 = (bf16[256,512]{1,0:T(8,128)(2,1)}, f32[256,512]{1,0:T(8,128)S(1)}, f32[256,512]{1,0:T(8,128)S(1)}, f32[8,128]{1,0:T(8,128)S(1)}) custom-call(s32[1,4]{1,0:T(1,128)S(1)} %copy-done.6, bf16[256,512]{1,0:T(8,128)(2,1)S(1)} %bitcast.27, bf16[256,512]{1,0:T(8,128)(2,1)S(1)} %bitcast.30, bf16[256,512]{1,0:T(8,128)(2,1)S(1)} %bitcast.34, ...), custom_call_target="tpu_custom_call" | custom-call | flops 356515840 | bytes 3145728 | tf_op jit(solution)/shard_map/pallas_call | solution.py:265
  74.2 4.3 %all-to-all-done.3 = f32[64,3,4,128]{3,2,1,0:T(4,128)S(1)} async-done(((f32[64,3,4,128]{3,2,1,0:T(4,128)}), f32[64,3,4,128]{3,2,1,0:T(4,128)S(1)}, u32[]{:S(2)}, u32[]{:S(2)}) %all-to-all-start.3) | async-done | bytes 393248 | tf_op jit(solution)/shard_map/all_to_all | solution.py:282
  78.5 0.8 shard_map.107
  79.4 12.8 %all-to-all-start.4 = ((f32[64,8,128]{2,1,0:T(8,128)}), f32[64,8,128]{2,1,0:T(8,128)S(1)}, u32[]{:S(2)}, u32[]{:S(2)}) async-start(f32[64,8,128]{2,1,0:T(8,128)} %bitcast.15), calls=%async_computation.4 | async-start | bytes 524288 | tf_op jit(solution)/shard_map/all_to_all | solution.py:282
  92.2 1.9 %collective-permute-start = (f32[4,128]{1,0:T(4,128)S(1)}, f32[4,128]{1,0:T(4,128)S(1)}, u32[]{:S(2)}, u32[]{:S(2)}) collective-permute-start(f32[4,128]{1,0:T(4,128)S(1)} %shard_map.108.part_ref), channel_id=1, source_target_pairs={{0,256},{256,0},{1,257},{257,1},{2,258},{258,2},{3,259},{259,3},{4... | collective-permute-start | bytes 6152 | tf_op jit(solution)/shard_map/ppermute | solution.py:383
  94.2 1.1 %collective-permute-done.other_ref = f32[4,128]{1,0:T(4,128)S(1)} collective-permute-done((f32[4,128]{1,0:T(4,128)S(1)}, f32[4,128]{1,0:T(4,128)S(1)}, u32[]{:S(2)}, u32[]{:S(2)}) %collective-permute-start) | collective-permute-done | bytes 2080 | tf_op jit(solution)/shard_map/ppermute | solution.py:383
  95.3 2.3 %all-to-all-done.4 = f32[64,8,128]{2,1,0:T(8,128)S(1)} async-done(((f32[64,8,128]{2,1,0:T(8,128)}), f32[64,8,128]{2,1,0:T(8,128)S(1)}, u32[]{:S(2)}, u32[]{:S(2)}) %all-to-all-start.4) | async-done | bytes 262176 | tf_op jit(solution)/shard_map/all_to_all | solution.py:282
  97.6 2.2 %shard_map.109 = (bf16[256,512]{1,0:T(8,128)(2,1)}, bf16[256,512]{1,0:T(8,128)(2,1)}, f32[4,128]{1,0:T(4,128)}) custom-call(s32[1,4]{1,0:T(1,128)S(1)} %copy-done.6, bf16[256,512]{1,0:T(8,128)(2,1)S(1)} %bitcast.31, bf16[256,512]{1,0:T(8,128)(2,1)S(1)} %bitcast.35, f32[512,128]{1,0:T(8,128)S(1)} %bitcast.39, f32[256,512]{1,0:T(8,128)S(1)} %get-tuple-element.33.gk_ref, ...), custom_call_target="tpu_custom_call" | custom-call | flops 71303168 | bytes 2097152 | tf_op jit(solution)/shard_map/pallas_call | solution.py:265
  (11 shorter events, 0.0 us)
Async XLA Ops:
  0.6 22.0 %copy-start.2 = (bf16[1,256,512]{2,1,0:T(8,128)(2,1)S(1)}, bf16[1,256,512]{2,1,0:T(8,128)(2,1)}, u32[]{:S(2)}) copy-start(bf16[1,256,512]{2,1,0:T(8,128)(2,1)} %param.8) | copy-start | bytes 786436
  0.6 22.0 %copy-start.3 = (bf16[1,256,512]{2,1,0:T(8,128)(2,1)S(1)}, bf16[1,256,512]{2,1,0:T(8,128)(2,1)}, u32[]{:S(2)}) copy-start(bf16[1,256,512]{2,1,0:T(8,128)(2,1)} %param.10) | copy-start | bytes 786436
  2.7 20.0 %copy-start = (bf16[1,256,512]{2,1,0:T(8,128)(2,1)S(1)}, bf16[1,256,512]{2,1,0:T(8,128)(2,1)}, u32[]{:S(2)}) copy-start(bf16[1,256,512]{2,1,0:T(8,128)(2,1)} %param.6) | copy-start | bytes 786436
  2.7 20.0 %copy-start.1 = (bf16[1,256,512]{2,1,0:T(8,128)(2,1)S(1)}, bf16[1,256,512]{2,1,0:T(8,128)(2,1)}, u32[]{:S(2)}) copy-start(bf16[1,256,512]{2,1,0:T(8,128)(2,1)} %param.7) | copy-start | bytes 786436
  2.8 26.8 %all-to-all-start = ((f32[64,9,1,128]{3,2,1,0:T(1,128)}), f32[64,9,1,128]{3,2,1,0:T(1,128)S(1)}, u32[]{:S(2)}, u32[]{:S(2)}) async-start(f32[64,9,1,128]{3,2,1,0:T(1,128)} %bitcast.46), calls=%async_computation | async-start | bytes 589824 | tf_op jit(solution)/shard_map/all_to_all | solution.py:282
  22.6 0.7 copy-start.7
  22.7 0.7 copy-start.6
  24.5 0.8 copy-start.4
  29.6 18.7 %copy-start.5 = (f32[256,512]{1,0:T(8,128)S(1)}, f32[256,512]{1,0:T(8,128)}, u32[]{:S(2)}) copy-start(f32[256,512]{1,0:T(8,128)} %copy-done.4) | copy-start | bytes 1572868
  58.7 19.8 %all-to-all-start.3 = ((f32[64,3,4,128]{3,2,1,0:T(4,128)}), f32[64,3,4,128]{3,2,1,0:T(4,128)S(1)}, u32[]{:S(2)}, u32[]{:S(2)}) async-start(f32[64,3,4,128]{3,2,1,0:T(4,128)} %bitcast.13), calls=%async_computation.3 | async-start | bytes 786432 | tf_op jit(solution)/shard_map/all_to_all | solution.py:282
  79.4 18.3 %all-to-all-start.4 = ((f32[64,8,128]{2,1,0:T(8,128)}), f32[64,8,128]{2,1,0:T(8,128)S(1)}, u32[]{:S(2)}, u32[]{:S(2)}) async-start(f32[64,8,128]{2,1,0:T(8,128)} %bitcast.15), calls=%async_computation.4 | async-start | bytes 524288 | tf_op jit(solution)/shard_map/all_to_all | solution.py:282
  92.2 3.1 %collective-permute-start = (f32[4,128]{1,0:T(4,128)S(1)}, f32[4,128]{1,0:T(4,128)S(1)}, u32[]{:S(2)}, u32[]{:S(2)}) collective-permute-start(f32[4,128]{1,0:T(4,128)S(1)} %shard_map.108.part_ref), channel_id=1, source_target_pairs={{0,256},{256,0},{1,257},{257,1},{2,258},{258,2},{3,259},{259,3},{4... | collective-permute-start | bytes 6152 | tf_op jit(solution)/shard_map/ppermute | solution.py:383

commit v3 on v2

--- a/solution.py
+++ b/solution.py
@@ -93,14 +93,13 @@
         copy.wait()
 
 
-def local_kernel(off_ref, q_ref, k_ref, v_ref, g_ref, gain_ref, out_ref, scaled_ref, token_ref):
+def local_kernel(off_ref, q_ref, k_ref, v_ref, gain_ref, out_ref, token_ref):
     length, width = q_ref.shape
     allowed = allowed_of(off_ref, length)
     for h in range(width // DH):
         scores = dot(q_ref[:, head(h)], k_ref[:, head(h)], 1, 1)
         weights = jnp.where(allowed, scores, 0.0).astype(BF16)
         out_ref[:, head(h)] = dot(weights, v_ref[:, head(h)], 1, 0)
-        scaled_ref[:, head(h)] = gain_ref[:, head(h)] * g_ref[:, head(h)].astype(F32)
     token_ref[...] = jnp.zeros_like(token_ref)
 
 
@@ -119,15 +118,18 @@
     return [order.index(w) for w in range(count)]
 
 
-def prefix_kernel(recv_ref, token_ref, send_ref):
+def prefix_kernel(recv_ref, token_ref, send_ref, keep_ref):
     carry = token_ref[...]
     for w in slots_of(recv_ref.shape[0] // 9):
         send_ref[8 * w : 8 * w + 8, :] = carry
-        keep = jnp.broadcast_to(recv_ref[9 * w + 8 : 9 * w + 9, :], (8, DH))
-        carry = recv_ref[9 * w : 9 * w + 8, :] + carry * keep
-
-
-def attend_kernel(off_ref, q_ref, local_ref, state_ref, scaled_ref, att_ref, sums_ref):
+        flag = recv_ref[9 * w + 8 : 9 * w + 9, :]
+        keep_ref[w : w + 1, :] = flag
+        carry = recv_ref[9 * w : 9 * w + 8, :] + carry * jnp.broadcast_to(flag, (8, DH))
+
+
+def attend_kernel(
+    off_ref, q_ref, local_ref, state_ref, g_ref, gain_ref, att_ref, sums_ref, carried_ref
+):
     length, width = q_ref.shape
     first, _, _ = bounds(off_ref)
     opened = row_mask(length, first=first)
@@ -135,11 +137,12 @@
     products = jnp.zeros((length, DH), F32)
     for h in range(width // DH):
         carried = state_ref[h * DH : (h + 1) * DH, :].astype(BF16)
+        carried_ref[h * DH : (h + 1) * DH, :] = carried
         carried_out = dot(q_ref[:, head(h)], carried, 1, 0)
         att = local_ref[:, head(h)] + jnp.where(opened, carried_out, 0.0)
         att_ref[:, head(h)] = att
         squares += att * att
-        products += scaled_ref[:, head(h)] * att
+        products += (gain_ref[:, head(h)] * g_ref[:, head(h)].astype(F32)) * att
     row = 0
     for total in (squares, products):
         for half in range(length // DH):
@@ -160,42 +163,25 @@
     return jnp.broadcast_to(inverse, (length, DH)), jnp.broadcast_to(mean, (length, DH))
 
 
-def pre_kernel(
-    off_ref, q_ref, att_ref, g_ref, scaled_ref, gain_ref, sums_ref,
-    pre_ref, out_hbm, send_hbm, out_ref, send_ref, sems,
-):
+def pre_kernel(off_ref, q_ref, att_ref, g_ref, gain_ref, sums_ref, pre_ref, send_ref):
     length, width = q_ref.shape
     first, _, _ = bounds(off_ref)
     opened = row_mask(length, first=first)
     inverse, mean = columns_of(sums_ref, length)
-    copies, parts, pres = [], [], []
+    parts = []
     for h in range(width // DH):
         normed = att_ref[:, head(h)] * inverse
-        out_ref[:, head(h)] = (gain_ref[:, head(h)] * normed).astype(BF16)
-        copies.append(
-            pltpu.make_async_copy(
-                out_ref.at[:, head(h)], out_hbm.at[:, head(h)], sems.at[0, h]
-            )
-        )
-        copies[-1].start()
-        pre = inverse * (scaled_ref[:, head(h)] - normed * mean)
+        upstream = g_ref[:, head(h)].astype(F32)
+        pre = inverse * (gain_ref[:, head(h)] * upstream - normed * mean)
         pre_ref[:, head(h)] = pre.astype(BF16)
-        pres.append(jnp.where(opened, pre, 0.0).astype(BF16))
-        upstream = g_ref[:, head(h)].astype(F32)
+        state = dot(q_ref[:, head(h)], jnp.where(opened, pre, 0.0).astype(BF16), 0, 0)
+        for j in range(DH // 8):
+            at = 12 * (h * (DH // 8) + j)
+            send_ref[at : at + 8, :] = state[8 * j : 8 * j + 8, :]
         parts.append(jnp.sum(upstream * normed, axis=0, keepdims=True))
     part = jnp.concatenate(parts, axis=0)
     for j in range(send_ref.shape[0] // 12):
         send_ref[12 * j + 8 : 12 * j + 12, :] = part
-    for h in range(width // DH):
-        state = dot(q_ref[:, head(h)], pres[h], 0, 0)
-        for j in range(DH // 8):
-            at = 12 * (h * (DH // 8) + j)
-            send_ref[at : at + 8, :] = state[8 * j : 8 * j + 8, :]
-        rows = slice(h * 12 * (DH // 8), (h + 1) * 12 * (DH // 8))
-        copies.append(pltpu.make_async_copy(send_ref.at[rows], send_hbm.at[rows], sems.at[1, h]))
-        copies[-1].start()
-    for copy in copies:
-        copy.wait()
 
 
 def suffix_kernel(flags_ref, recv_ref, token_ref, send_ref, after_ref):
@@ -203,7 +189,7 @@
     after_ref[...] = carry
     for w in reversed(slots_of(recv_ref.shape[0] // 12)):
         send_ref[8 * w : 8 * w + 8, :] = carry
-        keep = jnp.broadcast_to(flags_ref[9 * w + 8 : 9 * w + 9, :], (8, DH))
+        keep = jnp.broadcast_to(flags_ref[w : w + 1, :], (8, DH))
         carry = recv_ref[12 * w : 12 * w + 8, :] + carry * keep
 
 
@@ -215,9 +201,11 @@
 
 
 def grads_kernel(
-    off_ref, q_ref, k_ref, v_ref, pre_ref, state_ref, gq_ref, gk_ref, gv_ref, token_ref
+    off_ref, q_ref, k_ref, v_ref, pre_ref, carried_ref, att_ref, gain_ref, sums_ref,
+    gq_ref, gk_ref, gv_ref, out_ref, token_ref,
 ):
     length, width = q_ref.shape
+    inverse, _ = columns_of(sums_ref, length)
     token_ref[...] = jnp.zeros_like(token_ref)
     first, _, _ = bounds(off_ref)
     opened = row_mask(length, first=first)
@@ -230,35 +218,26 @@
         grad_scores = dot(pre, value, 1, 1)
         grad_weights = jnp.where(allowed, grad_scores, 0.0).astype(BF16)
         gk_ref[:, head(h)] = dot(grad_weights, query, 0, 0)
-        carried = state_ref[h * DH : (h + 1) * DH, :].astype(BF16)
+        out_ref[:, head(h)] = (gain_ref[:, head(h)] * (att_ref[:, head(h)] * inverse)).astype(BF16)
+        carried = carried_ref[h * DH : (h + 1) * DH, :]
         carried_grad = jnp.where(opened, dot(pre, carried, 1, 1), 0.0)
         gq_ref[:, head(h)] = (dot(grad_weights, key, 1, 0) + carried_grad).astype(BF16)
 
 
 def final_kernel(
     off_ref, k_ref, v_ref, later_ref, gk_ref, gv_ref, part_ref, other_ref,
-    outk_hbm, outv_hbm, gain_ref, outk, outv, sems,
+    outk_ref, outv_ref, gain_ref,
 ):
     length, width = k_ref.shape
     _, last, _ = bounds(off_ref)
     tail = row_mask(length, last=last)
-    copies = []
+    gain_ref[...] = part_ref[...] + other_ref[...]
     for h in range(width // DH):
         later = later_ref[h * DH : (h + 1) * DH, :].astype(BF16)
         from_values = jnp.where(tail, dot(v_ref[:, head(h)], later, 1, 1), 0.0)
         from_keys = jnp.where(tail, dot(k_ref[:, head(h)], later, 1, 0), 0.0)
-        outk[:, head(h)] = (gk_ref[:, head(h)] + from_values).astype(BF16)
-        outv[:, head(h)] = (gv_ref[:, head(h)] + from_keys).astype(BF16)
-        for i, (source, target) in enumerate(((outk, outk_hbm), (outv, outv_hbm))):
-            copies.append(
-                pltpu.make_async_copy(
-                    source.at[:, head(h)], target.at[:, head(h)], sems.at[i, h]
-                )
-            )
-            copies[-1].start()
-    gain_ref[...] = part_ref[...] + other_ref[...]
-    for copy in copies:
-        copy.wait()
+        outk_ref[:, head(h)] = (gk_ref[:, head(h)] + from_values).astype(BF16)
+        outv_ref[:, head(h)] = (gv_ref[:, head(h)] + from_keys).astype(BF16)
 
 
 def call(kernel, outs, flops, bytes_accessed, *args, ins=None, out_specs=None, scratch=(), grant=12):
@@ -317,49 +296,44 @@
     )
     tails = exchanged(tails, 9)
     token = (8, DH)
-    local, scaled, ready = call(
-        local_kernel,
-        [(wide, F32), (wide, F32), (token, F32)],
-        134 * mega,
+    local, ready = call(
+        local_kernel, [(wide, F32), (token, F32)], 134 * mega, mega, off, q, k, v, gain
+    )
+    prefixes, keep = call(
+        prefix_kernel, [((count * 8, DH), F32), ((count, DH), F32)], mega, mega, tails, ready
+    )
+    state = exchanged(prefixes, 8)
+    att, sums, carried = call(
+        attend_kernel,
+        [(wide, F32), ((16, DH), F32), ((width, DH), BF16)],
+        34 * mega,
         mega,
         off,
         q,
-        k,
-        v,
+        local,
+        state,
         g,
         gain,
-    )
-    (prefixes,) = call(prefix_kernel, [((count * 8, DH), F32)], mega, mega, tails, ready)
-    state = exchanged(prefixes, 8)
-    att, sums = call(
-        attend_kernel, [(wide, F32), ((16, DH), F32)], 34 * mega, mega, off, q, local, state, scaled
     )
     sums = lax.all_to_all(
         sums.reshape(4, 4, DH), "tensor", 0, 0, axis_index_groups=[[2, 3, 1, 0]]
     ).reshape(16, DH)
-    pre, out, grad_states = call(
+    pre, grad_states = call(
         pre_kernel,
-        [(wide, BF16), (wide, BF16), ((count * 12, DH), F32)],
+        [(wide, BF16), ((count * 12, DH), F32)],
         34 * mega,
         mega,
         off,
         q,
         att,
         g,
-        scaled,
         gain,
         sums,
-        out_specs=[VMEM, HBM, HBM],
-        scratch=(
-            pltpu.VMEM(wide, BF16),
-            pltpu.VMEM((count * 12, DH), F32),
-            dma((2, heads)),
-        ),
     )
     grad_states = exchanged(grad_states, 12)
-    gq, gk, gv, ready = call(
+    gq, gk, gv, out, ready = call(
         grads_kernel,
-        [(wide, BF16), (wide, F32), (wide, F32), (token, F32)],
+        [(wide, BF16), (wide, F32), (wide, F32), (wide, BF16), (token, F32)],
         340 * mega,
         3 * mega,
         off,
@@ -367,14 +341,17 @@
         k,
         v,
         pre,
-        state,
+        carried,
+        att,
+        gain,
+        sums,
     )
     suffixes, ready = call(
         suffix_kernel,
         [((count * 8, DH), F32), (token, F32)],
         mega,
         mega,
-        tails,
+        keep,
         grad_states,
         ready,
     )
@@ -394,8 +371,6 @@
         gv,
         part,
         other,
-        out_specs=[HBM, HBM, VMEM],
-        scratch=(pltpu.VMEM(wide, BF16), pltpu.VMEM(wide, BF16), dma((2, heads))),
     )
     return out[None], gq[None], gk[None], gv[None], gain_sum.reshape(width)
 

time: 100 us -> 99.7 us (level)
  no operation moved by 1% of the time
where the time goes in v3:
time: 99.7 us; the launch traced here: 99.2 us
  starting transfers between devices  47.3 us (47%)
  blocking collectives  26.2 us (26%)
  waiting for transfers between devices  12.7 us (13%)
  Pallas kernels  11.6 us (12%)
    all_to_all x3, starting transfers between devices, exchanged(): lax.all_to_all(rows.reshape((count, *tile, DH)), 'seq', 0, 0, axis_index_...  45.3 us
    all_to_all x1, blocking collectives, exchanged(): lax.all_to_all(rows.reshape((count, *tile, DH)), 'seq', 0, 0, axis_index_...  18.5 us
    pallas_call x9, Pallas kernels, call(): pl.pallas_call(kernel, out_shape=[jax.ShapeDtypeStruct(s, d) for s, d in...  11.6 us
    all_to_all x3, waiting for transfers between devices, exchanged(): lax.all_to_all(rows.reshape((count, *tile, DH)), 'seq', 0, 0, axis_index_...  11.6 us
    all_to_all x1, blocking collectives, shards(): lax.all_to_all(sums.reshape(4, 4, DH), 'tensor', 0, 0, axis_index_groups=...  7.69 us
  transfers between devices with their start and end apart: 4, of which 4 were waited for; matrix products, arithmetic and copies ran while one was open for 0% of the time, Pallas kernels for 4%

profile of v3, /device:TPU:2, one launch (start us, length us, event | category | flops | bytes accessed | tf_op | source)
XLA Modules:
  0.0 99.2 jit_solution(1377342209652437440)
XLA Ops:
  0.6 0.0 copy-start.2
  0.6 2.1 %shard_map.102 = f32[576,128]{1,0:T(8,128)} custom-call(s32[1,4]{1,0:T(1,128)} %off_ref.9, bf16[256,512]{1,0:T(8,128)(2,1)} %bitcast.24, bf16[256,512]{1,0:T(8,128)(2,1)} %bitcast.28), custom_call_target="tpu_custom_call" | custom-call | flops 35651584 | bytes 1048576 | tf_op jit(solution)/shard_map/pallas_call | solution.py:244
  2.7 0.0 copy-start
  2.7 0.0 copy-start.1
  2.7 19.9 %all-to-all-start = ((f32[64,9,1,128]{3,2,1,0:T(1,128)}), f32[64,9,1,128]{3,2,1,0:T(1,128)S(1)}, u32[]{:S(2)}, u32[]{:S(2)}) async-start(f32[64,9,1,128]{3,2,1,0:T(1,128)} %bitcast.47), calls=%async_computation | async-start | bytes 589824 | tf_op jit(solution)/shard_map/all_to_all | solution.py:261
  22.6 0.0 copy-start.4
  22.6 0.0 copy-start.5
  22.7 0.6 copy-done.4
  23.3 1.2 %shard_map.101 = (f32[256,512]{1,0:T(8,128)S(1)}, f32[8,128]{1,0:T(8,128)S(1)}) custom-call(s32[1,4]{1,0:T(1,128)S(1)} %copy-done.5, bf16[256,512]{1,0:T(8,128)(2,1)S(1)} %bitcast.20, bf16[256,512]{1,0:T(8,128)(2,1)S(1)} %bitcast.25, bf16[256,512]{1,0:T(8,128)(2,1)S(1)} %bitcast.29, f32[1,512]{1,0:T(1,128)S(1)} %bitcast.42), custom_call_target="tpu_custom_call" | custom-call | flops 140509184 | bytes 1048576 | tf_op jit(solution)/shard_map/pallas_call | solution.py:244
  24.5 5.1 %all-to-all-done = f32[64,9,1,128]{3,2,1,0:T(1,128)S(1)} async-done(((f32[64,9,1,128]{3,2,1,0:T(1,128)}), f32[64,9,1,128]{3,2,1,0:T(1,128)S(1)}, u32[]{:S(2)}, u32[]{:S(2)}) %all-to-all-start) | async-done | bytes 294944 | tf_op jit(solution)/shard_map/all_to_all | solution.py:261
  29.6 0.1 shard_map.103
  29.7 18.5 %all_to_all.25 = f32[64,8,128]{2,1,0:T(8,128)S(1)} all-to-all(f32[64,8,128]{2,1,0:T(8,128)S(1)} %bitcast.39), channel_id=1, replica_groups={{144,0,4,28,32,224,8,24,36,60,64,192,228,252,12,20,40,56,68,92,96,160,1..., dimensions={0} | all-to-all | bytes 524288 | tf_op jit(solution)/shard_map/all_to_all | solution.py:261
  48.2 0.9 shard_map.104
  49.2 7.7 %all_to_all.26 = f32[4,4,128]{2,1,0:T(4,128)S(1)} all-to-all(f32[4,4,128]{2,1,0:T(4,128)S(1)} %bitcast.46), channel_id=1, replica_groups={{2,3,1,0},{6,7,5,4},{10,11,9,8},{14,15,13,12},{18,19,17,16},{22,23,21,2..., dimensions={0} | all-to-all | bytes 16384 | tf_op jit(solution)/shard_map/all_to_all | solution.py:318
  56.8 1.9 %shard_map.105 = (bf16[256,512]{1,0:T(8,128)(2,1)S(1)}, f32[768,128]{1,0:T(8,128)}) custom-call(s32[1,4]{1,0:T(1,128)S(1)} %copy-done.5, bf16[256,512]{1,0:T(8,128)(2,1)S(1)} %bitcast.22, f32[256,512]{1,0:T(8,128)S(1)} %get-tuple-element.27.att_ref, bf16[256,512]{1,0:T(8,128)(2,1)S(1)} %bitcast.37, f32[1,512]{1,0:T(1,128)S(1)} %bitcast.44, ...), custom_call_target="tpu_custom_call" | custom-call | flops 35651584 | bytes 1048576 | tf_op jit(solution)/shard_map/pallas_call | solution.py:244
  58.7 12.6 %all-to-all-start.3 = ((f32[64,3,4,128]{3,2,1,0:T(4,128)}), f32[64,3,4,128]{3,2,1,0:T(4,128)S(1)}, u32[]{:S(2)}, u32[]{:S(2)}) async-start(f32[64,3,4,128]{3,2,1,0:T(4,128)} %bitcast.13), calls=%async_computation.3 | async-start | bytes 786432 | tf_op jit(solution)/shard_map/all_to_all | solution.py:261
  71.4 3.0 %shard_map.106 = (bf16[256,512]{1,0:T(8,128)(2,1)}, f32[256,512]{1,0:T(8,128)S(1)}, f32[256,512]{1,0:T(8,128)S(1)}, bf16[256,512]{1,0:T(8,128)(2,1)}, f32[8,128]{1,0:T(8,128)S(1)}) custom-call(s32[1,4]{1,0:T(1,128)S(1)} %copy-done.5, bf16[256,512]{1,0:T(8,128)(2,1)S(1)} %bitcast.23, bf16[256,512]{1,0:T(8,128)(2,1)S(1)} %bitcast.26, ...), custom_call_target="tpu_custom_call" | custom-call | flops 356515840 | bytes 3145728 | tf_op jit(solution)/shard_map/pallas_call | solution.py:244
  74.3 4.2 %all-to-all-done.3 = f32[64,3,4,128]{3,2,1,0:T(4,128)S(1)} async-done(((f32[64,3,4,128]{3,2,1,0:T(4,128)}), f32[64,3,4,128]{3,2,1,0:T(4,128)S(1)}, u32[]{:S(2)}, u32[]{:S(2)}) %all-to-all-start.3) | async-done | bytes 393248 | tf_op jit(solution)/shard_map/all_to_all | solution.py:261
  78.5 0.8 shard_map.107
  79.3 12.8 %all-to-all-start.4 = ((f32[64,8,128]{2,1,0:T(8,128)}), f32[64,8,128]{2,1,0:T(8,128)S(1)}, u32[]{:S(2)}, u32[]{:S(2)}) async-start(f32[64,8,128]{2,1,0:T(8,128)} %bitcast.15), calls=%async_computation.4 | async-start | bytes 524288 | tf_op jit(solution)/shard_map/all_to_all | solution.py:261
  92.2 1.9 %collective-permute-start = (f32[4,128]{1,0:T(4,128)S(1)}, f32[4,128]{1,0:T(4,128)S(1)}, u32[]{:S(2)}, u32[]{:S(2)}) collective-permute-start(f32[4,128]{1,0:T(4,128)S(1)} %shard_map.108.part_ref), channel_id=1, source_target_pairs={{0,256},{256,0},{1,257},{257,1},{2,258},{258,2},{3,259},{259,3},{4... | collective-permute-start | bytes 6152 | tf_op jit(solution)/shard_map/ppermute | solution.py:360
  94.1 1.1 %collective-permute-done.other_ref = f32[4,128]{1,0:T(4,128)S(1)} collective-permute-done((f32[4,128]{1,0:T(4,128)S(1)}, f32[4,128]{1,0:T(4,128)S(1)}, u32[]{:S(2)}, u32[]{:S(2)}) %collective-permute-start) | collective-permute-done | bytes 2080 | tf_op jit(solution)/shard_map/ppermute | solution.py:360
  95.3 2.3 %all-to-all-done.4 = f32[64,8,128]{2,1,0:T(8,128)S(1)} async-done(((f32[64,8,128]{2,1,0:T(8,128)}), f32[64,8,128]{2,1,0:T(8,128)S(1)}, u32[]{:S(2)}, u32[]{:S(2)}) %all-to-all-start.4) | async-done | bytes 262176 | tf_op jit(solution)/shard_map/all_to_all | solution.py:261
  97.6 1.6 %shard_map.109 = (bf16[256,512]{1,0:T(8,128)(2,1)}, bf16[256,512]{1,0:T(8,128)(2,1)}, f32[4,128]{1,0:T(4,128)}) custom-call(s32[1,4]{1,0:T(1,128)S(1)} %copy-done.5, bf16[256,512]{1,0:T(8,128)(2,1)S(1)} %bitcast.27, bf16[256,512]{1,0:T(8,128)(2,1)S(1)} %bitcast.31, f32[512,128]{1,0:T(8,128)S(1)} %bitcast.38, f32[256,512]{1,0:T(8,128)S(1)} %get-tuple-element.37.gk_ref, ...), custom_call_target="tpu_custom_call" | custom-call | flops 71303168 | bytes 2097152 | tf_op jit(solution)/shard_map/pallas_call | solution.py:244
  (7 shorter events, 0.0 us)
Async XLA Ops:
  0.6 22.0 %copy-start.2 = (bf16[1,256,512]{2,1,0:T(8,128)(2,1)S(1)}, bf16[1,256,512]{2,1,0:T(8,128)(2,1)}, u32[]{:S(2)}) copy-start(bf16[1,256,512]{2,1,0:T(8,128)(2,1)} %param.8) | copy-start | bytes 786436
  2.7 19.9 %copy-start = (bf16[1,256,512]{2,1,0:T(8,128)(2,1)S(1)}, bf16[1,256,512]{2,1,0:T(8,128)(2,1)}, u32[]{:S(2)}) copy-start(bf16[1,256,512]{2,1,0:T(8,128)(2,1)} %param.6) | copy-start | bytes 786436
  2.7 19.9 %copy-start.1 = (bf16[1,256,512]{2,1,0:T(8,128)(2,1)S(1)}, bf16[1,256,512]{2,1,0:T(8,128)(2,1)}, u32[]{:S(2)}) copy-start(bf16[1,256,512]{2,1,0:T(8,128)(2,1)} %param.7) | copy-start | bytes 786436
  2.7 26.8 %all-to-all-start = ((f32[64,9,1,128]{3,2,1,0:T(1,128)}), f32[64,9,1,128]{3,2,1,0:T(1,128)S(1)}, u32[]{:S(2)}, u32[]{:S(2)}) async-start(f32[64,9,1,128]{3,2,1,0:T(1,128)} %bitcast.47), calls=%async_computation | async-start | bytes 589824 | tf_op jit(solution)/shard_map/all_to_all | solution.py:261
  22.6 0.7 copy-start.4
  22.6 0.7 copy-start.5
  29.7 18.5 %copy-start.3 = (bf16[1,256,512]{2,1,0:T(8,128)(2,1)S(1)}, bf16[1,256,512]{2,1,0:T(8,128)(2,1)}, u32[]{:S(2)}) copy-start(bf16[1,256,512]{2,1,0:T(8,128)(2,1)} %param.10) | copy-start | bytes 786436
  58.7 19.8 %all-to-all-start.3 = ((f32[64,3,4,128]{3,2,1,0:T(4,128)}), f32[64,3,4,128]{3,2,1,0:T(4,128)S(1)}, u32[]{:S(2)}, u32[]{:S(2)}) async-start(f32[64,3,4,128]{3,2,1,0:T(4,128)} %bitcast.13), calls=%async_computation.3 | async-start | bytes 786432 | tf_op jit(solution)/shard_map/all_to_all | solution.py:261
  79.3 18.3 %all-to-all-start.4 = ((f32[64,8,128]{2,1,0:T(8,128)}), f32[64,8,128]{2,1,0:T(8,128)S(1)}, u32[]{:S(2)}, u32[]{:S(2)}) async-start(f32[64,8,128]{2,1,0:T(8,128)} %bitcast.15), calls=%async_computation.4 | async-start | bytes 524288 | tf_op jit(solution)/shard_map/all_to_all | solution.py:261
  92.2 3.1 %collective-permute-start = (f32[4,128]{1,0:T(4,128)S(1)}, f32[4,128]{1,0:T(4,128)S(1)}, u32[]{:S(2)}, u32[]{:S(2)}) collective-permute-start(f32[4,128]{1,0:T(4,128)S(1)} %shard_map.108.part_ref), channel_id=1, source_target_pairs={{0,256},{256,0},{1,257},{257,1},{2,258},{258,2},{3,259},{259,3},{4... | collective-permute-start | bytes 6152 | tf_op jit(solution)/shard_map/ppermute | solution.py:360

commit v4 on v3

--- a/solution.py
+++ b/solution.py
@@ -9,7 +9,7 @@
 BLK = 64
 CH = 2048
 EPS = 1e-05
-ROOT = 36
+ROOT = 37
 VMEM = pl.BlockSpec(memory_space=pltpu.VMEM)
 SMEM = pl.BlockSpec(memory_space=pltpu.SMEM)
 HBM = pl.BlockSpec(memory_space=pltpu.HBM)

time: 99.7 us -> 99.3 us (level)
  starting transfers between devices: 47.3 us -> 44.6 us
  waiting for transfers between devices: 12.7 us -> 15.2 us
    all_to_all x3, starting transfers between devices: 45.3 us -> 42.7 us  [exchanged(): lax.all_to_all(rows.reshape((count, *tile, DH)), 'seq', 0, 0, axis_index_...]
    all_to_all x3, waiting for transfers between devices: 11.6 us -> 14.1 us  [exchanged(): lax.all_to_all(rows.reshape((count, *tile, DH)), 'seq', 0, 0, axis_index_...]
where the time goes in v4:
time: 99.3 us; the launch traced here: 98.8 us
  starting transfers between devices  44.6 us (45%)
  blocking collectives  26 us (26%)
  waiting for transfers between devices  15.2 us (15%)
  Pallas kernels  11.6 us (12%)
    all_to_all x3, starting transfers between devices, exchanged(): lax.all_to_all(rows.reshape((count, *tile, DH)), 'seq', 0, 0, axis_index_...  42.7 us
    all_to_all x1, blocking collectives, exchanged(): lax.all_to_all(rows.reshape((count, *tile, DH)), 'seq', 0, 0, axis_index_...  18.3 us
    all_to_all x3, waiting for transfers between devices, exchanged(): lax.all_to_all(rows.reshape((count, *tile, DH)), 'seq', 0, 0, axis_index_...  14.1 us
    pallas_call x9, Pallas kernels, call(): pl.pallas_call(kernel, out_shape=[jax.ShapeDtypeStruct(s, d) for s, d in...  11.6 us
    all_to_all x1, blocking collectives, shards(): lax.all_to_all(sums.reshape(4, 4, DH), 'tensor', 0, 0, axis_index_groups=...  7.69 us
  transfers between devices with their start and end apart: 4, of which 4 were waited for; matrix products, arithmetic and copies ran while one was open for 0% of the time, Pallas kernels for 4%

profile of v4, /device:TPU:2, one launch (start us, length us, event | category | flops | bytes accessed | tf_op | source)
XLA Modules:
  0.0 98.8 jit_solution(14160938665389220995)
XLA Ops:
  0.6 0.0 copy-start.2
  0.6 2.1 %shard_map.102 = f32[576,128]{1,0:T(8,128)} custom-call(s32[1,4]{1,0:T(1,128)} %off_ref.9, bf16[256,512]{1,0:T(8,128)(2,1)} %bitcast.24, bf16[256,512]{1,0:T(8,128)(2,1)} %bitcast.28), custom_call_target="tpu_custom_call" | custom-call | flops 35651584 | bytes 1048576 | tf_op jit(solution)/shard_map/pallas_call | solution.py:244
  2.7 0.0 copy-start
  2.7 0.0 copy-start.1
  2.7 19.0 %all-to-all-start = ((f32[64,9,1,128]{3,2,1,0:T(1,128)}), f32[64,9,1,128]{3,2,1,0:T(1,128)S(1)}, u32[]{:S(2)}, u32[]{:S(2)}) async-start(f32[64,9,1,128]{3,2,1,0:T(1,128)} %bitcast.47), calls=%async_computation | async-start | bytes 589824 | tf_op jit(solution)/shard_map/all_to_all | solution.py:261
  21.7 0.0 copy-start.4
  21.7 0.0 copy-start.5
  21.8 0.6 copy-done.4
  22.4 1.2 %shard_map.101 = (f32[256,512]{1,0:T(8,128)S(1)}, f32[8,128]{1,0:T(8,128)S(1)}) custom-call(s32[1,4]{1,0:T(1,128)S(1)} %copy-done.5, bf16[256,512]{1,0:T(8,128)(2,1)S(1)} %bitcast.20, bf16[256,512]{1,0:T(8,128)(2,1)S(1)} %bitcast.25, bf16[256,512]{1,0:T(8,128)(2,1)S(1)} %bitcast.29, f32[1,512]{1,0:T(1,128)S(1)} %bitcast.42), custom_call_target="tpu_custom_call" | custom-call | flops 140509184 | bytes 1048576 | tf_op jit(solution)/shard_map/pallas_call | solution.py:244
  23.6 6.0 %all-to-all-done = f32[64,9,1,128]{3,2,1,0:T(1,128)S(1)} async-done(((f32[64,9,1,128]{3,2,1,0:T(1,128)}), f32[64,9,1,128]{3,2,1,0:T(1,128)S(1)}, u32[]{:S(2)}, u32[]{:S(2)}) %all-to-all-start) | async-done | bytes 294944 | tf_op jit(solution)/shard_map/all_to_all | solution.py:261
  29.6 0.1 shard_map.103
  29.7 18.3 %all_to_all.25 = f32[64,8,128]{2,1,0:T(8,128)S(1)} all-to-all(f32[64,8,128]{2,1,0:T(8,128)S(1)} %bitcast.39), channel_id=1, replica_groups={{148,4,0,8,36,228,12,28,32,40,68,196,224,232,16,24,44,60,64,72,100,164,..., dimensions={0} | all-to-all | bytes 524288 | tf_op jit(solution)/shard_map/all_to_all | solution.py:261
  48.0 0.9 shard_map.104
  49.0 7.7 %all_to_all.26 = f32[4,4,128]{2,1,0:T(4,128)S(1)} all-to-all(f32[4,4,128]{2,1,0:T(4,128)S(1)} %bitcast.46), channel_id=1, replica_groups={{2,3,1,0},{6,7,5,4},{10,11,9,8},{14,15,13,12},{18,19,17,16},{22,23,21,2..., dimensions={0} | all-to-all | bytes 16384 | tf_op jit(solution)/shard_map/all_to_all | solution.py:318
  56.6 1.9 %shard_map.105 = (bf16[256,512]{1,0:T(8,128)(2,1)S(1)}, f32[768,128]{1,0:T(8,128)}) custom-call(s32[1,4]{1,0:T(1,128)S(1)} %copy-done.5, bf16[256,512]{1,0:T(8,128)(2,1)S(1)} %bitcast.22, f32[256,512]{1,0:T(8,128)S(1)} %get-tuple-element.27.att_ref, bf16[256,512]{1,0:T(8,128)(2,1)S(1)} %bitcast.37, f32[1,512]{1,0:T(1,128)S(1)} %bitcast.44, ...), custom_call_target="tpu_custom_call" | custom-call | flops 35651584 | bytes 1048576 | tf_op jit(solution)/shard_map/pallas_call | solution.py:244
  58.5 11.9 %all-to-all-start.3 = ((f32[64,3,4,128]{3,2,1,0:T(4,128)}), f32[64,3,4,128]{3,2,1,0:T(4,128)S(1)}, u32[]{:S(2)}, u32[]{:S(2)}) async-start(f32[64,3,4,128]{3,2,1,0:T(4,128)} %bitcast.13), calls=%async_computation.3 | async-start | bytes 786432 | tf_op jit(solution)/shard_map/all_to_all | solution.py:261
  70.4 3.0 %shard_map.106 = (bf16[256,512]{1,0:T(8,128)(2,1)}, f32[256,512]{1,0:T(8,128)S(1)}, f32[256,512]{1,0:T(8,128)S(1)}, bf16[256,512]{1,0:T(8,128)(2,1)}, f32[8,128]{1,0:T(8,128)S(1)}) custom-call(s32[1,4]{1,0:T(1,128)S(1)} %copy-done.5, bf16[256,512]{1,0:T(8,128)(2,1)S(1)} %bitcast.23, bf16[256,512]{1,0:T(8,128)(2,1)S(1)} %bitcast.26, ...), custom_call_target="tpu_custom_call" | custom-call | flops 356515840 | bytes 3145728 | tf_op jit(solution)/shard_map/pallas_call | solution.py:244
  73.4 5.4 %all-to-all-done.3 = f32[64,3,4,128]{3,2,1,0:T(4,128)S(1)} async-done(((f32[64,3,4,128]{3,2,1,0:T(4,128)}), f32[64,3,4,128]{3,2,1,0:T(4,128)S(1)}, u32[]{:S(2)}, u32[]{:S(2)}) %all-to-all-start.3) | async-done | bytes 393248 | tf_op jit(solution)/shard_map/all_to_all | solution.py:261
  78.8 0.8 shard_map.107
  79.6 11.8 %all-to-all-start.4 = ((f32[64,8,128]{2,1,0:T(8,128)}), f32[64,8,128]{2,1,0:T(8,128)S(1)}, u32[]{:S(2)}, u32[]{:S(2)}) async-start(f32[64,8,128]{2,1,0:T(8,128)} %bitcast.15), calls=%async_computation.4 | async-start | bytes 524288 | tf_op jit(solution)/shard_map/all_to_all | solution.py:261
  91.4 1.9 %collective-permute-start = (f32[4,128]{1,0:T(4,128)S(1)}, f32[4,128]{1,0:T(4,128)S(1)}, u32[]{:S(2)}, u32[]{:S(2)}) collective-permute-start(f32[4,128]{1,0:T(4,128)S(1)} %shard_map.108.part_ref), channel_id=1, source_target_pairs={{0,256},{256,0},{1,257},{257,1},{2,258},{258,2},{3,259},{259,3},{4... | collective-permute-start | bytes 6152 | tf_op jit(solution)/shard_map/ppermute | solution.py:360
  93.4 1.1 %collective-permute-done.other_ref = f32[4,128]{1,0:T(4,128)S(1)} collective-permute-done((f32[4,128]{1,0:T(4,128)S(1)}, f32[4,128]{1,0:T(4,128)S(1)}, u32[]{:S(2)}, u32[]{:S(2)}) %collective-permute-start) | collective-permute-done | bytes 2080 | tf_op jit(solution)/shard_map/ppermute | solution.py:360
  94.5 2.7 %all-to-all-done.4 = f32[64,8,128]{2,1,0:T(8,128)S(1)} async-done(((f32[64,8,128]{2,1,0:T(8,128)}), f32[64,8,128]{2,1,0:T(8,128)S(1)}, u32[]{:S(2)}, u32[]{:S(2)}) %all-to-all-start.4) | async-done | bytes 262176 | tf_op jit(solution)/shard_map/all_to_all | solution.py:261
  97.2 1.6 %shard_map.109 = (bf16[256,512]{1,0:T(8,128)(2,1)}, bf16[256,512]{1,0:T(8,128)(2,1)}, f32[4,128]{1,0:T(4,128)}) custom-call(s32[1,4]{1,0:T(1,128)S(1)} %copy-done.5, bf16[256,512]{1,0:T(8,128)(2,1)S(1)} %bitcast.27, bf16[256,512]{1,0:T(8,128)(2,1)S(1)} %bitcast.31, f32[512,128]{1,0:T(8,128)S(1)} %bitcast.38, f32[256,512]{1,0:T(8,128)S(1)} %get-tuple-element.37.gk_ref, ...), custom_call_target="tpu_custom_call" | custom-call | flops 71303168 | bytes 2097152 | tf_op jit(solution)/shard_map/pallas_call | solution.py:244
  (7 shorter events, 0.0 us)
Async XLA Ops:
  0.6 21.1 %copy-start.2 = (bf16[1,256,512]{2,1,0:T(8,128)(2,1)S(1)}, bf16[1,256,512]{2,1,0:T(8,128)(2,1)}, u32[]{:S(2)}) copy-start(bf16[1,256,512]{2,1,0:T(8,128)(2,1)} %param.8) | copy-start | bytes 786436
  2.7 19.0 %copy-start = (bf16[1,256,512]{2,1,0:T(8,128)(2,1)S(1)}, bf16[1,256,512]{2,1,0:T(8,128)(2,1)}, u32[]{:S(2)}) copy-start(bf16[1,256,512]{2,1,0:T(8,128)(2,1)} %param.6) | copy-start | bytes 786436
  2.7 19.0 %copy-start.1 = (bf16[1,256,512]{2,1,0:T(8,128)(2,1)S(1)}, bf16[1,256,512]{2,1,0:T(8,128)(2,1)}, u32[]{:S(2)}) copy-start(bf16[1,256,512]{2,1,0:T(8,128)(2,1)} %param.7) | copy-start | bytes 786436
  2.7 26.9 %all-to-all-start = ((f32[64,9,1,128]{3,2,1,0:T(1,128)}), f32[64,9,1,128]{3,2,1,0:T(1,128)S(1)}, u32[]{:S(2)}, u32[]{:S(2)}) async-start(f32[64,9,1,128]{3,2,1,0:T(1,128)} %bitcast.47), calls=%async_computation | async-start | bytes 589824 | tf_op jit(solution)/shard_map/all_to_all | solution.py:261
  21.7 0.7 copy-start.4
  21.7 0.7 copy-start.5
  29.7 18.3 %copy-start.3 = (bf16[1,256,512]{2,1,0:T(8,128)(2,1)S(1)}, bf16[1,256,512]{2,1,0:T(8,128)(2,1)}, u32[]{:S(2)}) copy-start(bf16[1,256,512]{2,1,0:T(8,128)(2,1)} %param.10) | copy-start | bytes 786436
  58.5 20.2 %all-to-all-start.3 = ((f32[64,3,4,128]{3,2,1,0:T(4,128)}), f32[64,3,4,128]{3,2,1,0:T(4,128)S(1)}, u32[]{:S(2)}, u32[]{:S(2)}) async-start(f32[64,3,4,128]{3,2,1,0:T(4,128)} %bitcast.13), calls=%async_computation.3 | async-start | bytes 786432 | tf_op jit(solution)/shard_map/all_to_all | solution.py:261
  79.6 17.6 %all-to-all-start.4 = ((f32[64,8,128]{2,1,0:T(8,128)}), f32[64,8,128]{2,1,0:T(8,128)S(1)}, u32[]{:S(2)}, u32[]{:S(2)}) async-start(f32[64,8,128]{2,1,0:T(8,128)} %bitcast.15), calls=%async_computation.4 | async-start | bytes 524288 | tf_op jit(solution)/shard_map/all_to_all | solution.py:261
  91.4 3.1 %collective-permute-start = (f32[4,128]{1,0:T(4,128)S(1)}, f32[4,128]{1,0:T(4,128)S(1)}, u32[]{:S(2)}, u32[]{:S(2)}) collective-permute-start(f32[4,128]{1,0:T(4,128)S(1)} %shard_map.108.part_ref), channel_id=1, source_target_pairs={{0,256},{256,0},{1,257},{257,1},{2,258},{258,2},{3,259},{259,3},{4... | collective-permute-start | bytes 6152 | tf_op jit(solution)/shard_map/ppermute | solution.py:360

commit v5 on v4

--- a/solution.py
+++ b/solution.py
@@ -93,13 +93,17 @@
         copy.wait()
 
 
-def local_kernel(off_ref, q_ref, k_ref, v_ref, gain_ref, out_ref, token_ref):
+def local_kernel(off_ref, q_ref, k_ref, v_ref, gain_ref, out_ref, turned_ref, token_ref):
     length, width = q_ref.shape
+    first, _, _ = bounds(off_ref)
+    opened = row_mask(length, first=first)
     allowed = allowed_of(off_ref, length)
     for h in range(width // DH):
         scores = dot(q_ref[:, head(h)], k_ref[:, head(h)], 1, 1)
         weights = jnp.where(allowed, scores, 0.0).astype(BF16)
         out_ref[:, head(h)] = dot(weights, v_ref[:, head(h)], 1, 0)
+        query = jnp.where(opened, q_ref[:, head(h)], jnp.zeros((), BF16))
+        turned_ref[h * DH : (h + 1) * DH, :] = query.T
     token_ref[...] = jnp.zeros_like(token_ref)
 
 
@@ -157,24 +161,25 @@
     halves = length // DH
     inv = lax.rsqrt(total[0:halves, :] / CH + EPS)
     mean = inv * total[halves : 2 * halves, :] / CH
-    cols = jnp.concatenate([inv, mean, inv, mean], axis=0).T
-    inverse = jnp.concatenate([cols[:, i : i + 1] for i in range(halves)], axis=0)
-    mean = jnp.concatenate([cols[:, halves + i : halves + i + 1] for i in range(halves)], axis=0)
-    return jnp.broadcast_to(inverse, (length, DH)), jnp.broadcast_to(mean, (length, DH))
-
-
-def pre_kernel(off_ref, q_ref, att_ref, g_ref, gain_ref, sums_ref, pre_ref, send_ref):
-    length, width = q_ref.shape
-    first, _, _ = bounds(off_ref)
-    opened = row_mask(length, first=first)
+
+    def column(rows):
+        blocks = [jnp.broadcast_to(rows[i : i + 1], (DH, DH)).T for i in range(halves)]
+        return jnp.concatenate(blocks, axis=0)
+
+    return column(inv), column(mean)
+
+
+def pre_kernel(turned_ref, att_ref, g_ref, gain_ref, sums_ref, pre_ref, send_ref):
+    length, width = att_ref.shape
     inverse, mean = columns_of(sums_ref, length)
     parts = []
     for h in range(width // DH):
         normed = att_ref[:, head(h)] * inverse
         upstream = g_ref[:, head(h)].astype(F32)
         pre = inverse * (gain_ref[:, head(h)] * upstream - normed * mean)
-        pre_ref[:, head(h)] = pre.astype(BF16)
-        state = dot(q_ref[:, head(h)], jnp.where(opened, pre, 0.0).astype(BF16), 0, 0)
+        rounded = pre.astype(BF16)
+        pre_ref[:, head(h)] = rounded
+        state = dot(turned_ref[h * DH : (h + 1) * DH, :], rounded, 1, 0)
         for j in range(DH // 8):
             at = 12 * (h * (DH // 8) + j)
             send_ref[at : at + 8, :] = state[8 * j : 8 * j + 8, :]
@@ -296,8 +301,16 @@
     )
     tails = exchanged(tails, 9)
     token = (8, DH)
-    local, ready = call(
-        local_kernel, [(wide, F32), (token, F32)], 134 * mega, mega, off, q, k, v, gain
+    local, turned, ready = call(
+        local_kernel,
+        [(wide, F32), ((width, length), BF16), (token, F32)],
+        134 * mega,
+        mega,
+        off,
+        q,
+        k,
+        v,
+        gain,
     )
     prefixes, keep = call(
         prefix_kernel, [((count * 8, DH), F32), ((count, DH), F32)], mega, mega, tails, ready
@@ -323,8 +336,7 @@
         [(wide, BF16), ((count * 12, DH), F32)],
         34 * mega,
         mega,
-        off,
-        q,
+        turned,
         att,
         g,
         gain,

time: 99.3 us -> 98.6 us (level)
  no operation moved by 1% of the time
where the time goes in v5:
time: 98.6 us; the launch traced here: 98.1 us
  starting transfers between devices  44.6 us (45%)
  blocking collectives  26 us (26%)
  waiting for transfers between devices  15.2 us (15%)
  Pallas kernels  10.9 us (11%)
    all_to_all x3, starting transfers between devices, exchanged(): lax.all_to_all(rows.reshape((count, *tile, DH)), 'seq', 0, 0, axis_index_...  42.7 us
    all_to_all x1, blocking collectives, exchanged(): lax.all_to_all(rows.reshape((count, *tile, DH)), 'seq', 0, 0, axis_index_...  18.3 us
    all_to_all x3, waiting for transfers between devices, exchanged(): lax.all_to_all(rows.reshape((count, *tile, DH)), 'seq', 0, 0, axis_index_...  14.1 us
    pallas_call x9, Pallas kernels, call(): pl.pallas_call(kernel, out_shape=[jax.ShapeDtypeStruct(s, d) for s, d in...  10.9 us
    all_to_all x1, blocking collectives, shards(): lax.all_to_all(sums.reshape(4, 4, DH), 'tensor', 0, 0, axis_index_groups=...  7.69 us
  transfers between devices with their start and end apart: 4, of which 4 were waited for; matrix products, arithmetic and copies ran while one was open for 0% of the time, Pallas kernels for 4%

profile of v5, /device:TPU:2, one launch (start us, length us, event | category | flops | bytes accessed | tf_op | source)
XLA Modules:
  0.0 98.1 jit_solution(14756743427921148330)
XLA Ops:
  0.6 0.0 copy-start.2
  0.6 2.1 %shard_map.102 = f32[576,128]{1,0:T(8,128)} custom-call(s32[1,4]{1,0:T(1,128)} %off_ref.7, bf16[256,512]{1,0:T(8,128)(2,1)} %bitcast.20, bf16[256,512]{1,0:T(8,128)(2,1)} %bitcast.24), custom_call_target="tpu_custom_call" | custom-call | flops 35651584 | bytes 1048576 | tf_op jit(solution)/shard_map/pallas_call | solution.py:249
  2.7 0.0 copy-start
  2.7 0.0 copy-start.1
  2.7 19.0 %all-to-all-start = ((f32[64,9,1,128]{3,2,1,0:T(1,128)}), f32[64,9,1,128]{3,2,1,0:T(1,128)S(1)}, u32[]{:S(2)}, u32[]{:S(2)}) async-start(f32[64,9,1,128]{3,2,1,0:T(1,128)} %bitcast.46), calls=%async_computation | async-start | bytes 589824 | tf_op jit(solution)/shard_map/all_to_all | solution.py:266
  21.7 0.0 copy-start.4
  21.7 0.0 copy-start.5
  21.8 0.6 copy-done.4
  22.4 1.2 %shard_map.101 = (f32[256,512]{1,0:T(8,128)S(1)}, bf16[512,256]{1,0:T(8,128)(2,1)S(1)}, f32[8,128]{1,0:T(8,128)S(1)}) custom-call(s32[1,4]{1,0:T(1,128)S(1)} %copy-done.5, bf16[256,512]{1,0:T(8,128)(2,1)S(1)} %bitcast.30, bf16[256,512]{1,0:T(8,128)(2,1)S(1)} %bitcast.21, bf16[256,512]{1,0:T(8,128)(2,1)S(1)} %bitcast.25, f32[1,512]{1,0:T(1,128)S(1)} %bitcast.41), custom_call_target="tpu_custom_call" | custom-call | flops 140509184 | bytes 1048576 | tf_op jit(solution)/shard_map/pallas_call | solution.py:249
  23.6 6.0 %all-to-all-done = f32[64,9,1,128]{3,2,1,0:T(1,128)S(1)} async-done(((f32[64,9,1,128]{3,2,1,0:T(1,128)}), f32[64,9,1,128]{3,2,1,0:T(1,128)S(1)}, u32[]{:S(2)}, u32[]{:S(2)}) %all-to-all-start) | async-done | bytes 294944 | tf_op jit(solution)/shard_map/all_to_all | solution.py:266
  29.6 0.1 shard_map.103
  29.7 18.3 %all_to_all.25 = f32[64,8,128]{2,1,0:T(8,128)S(1)} all-to-all(f32[64,8,128]{2,1,0:T(8,128)S(1)} %bitcast.38), channel_id=1, replica_groups={{148,4,0,8,36,228,12,28,32,40,68,196,224,232,16,24,44,60,64,72,100,164,..., dimensions={0} | all-to-all | bytes 524288 | tf_op jit(solution)/shard_map/all_to_all | solution.py:266
  48.0 0.9 shard_map.104
  49.0 7.7 %all_to_all.26 = f32[4,4,128]{2,1,0:T(4,128)S(1)} all-to-all(f32[4,4,128]{2,1,0:T(4,128)S(1)} %bitcast.45), channel_id=1, replica_groups={{2,3,1,0},{6,7,5,4},{10,11,9,8},{14,15,13,12},{18,19,17,16},{22,23,21,2..., dimensions={0} | all-to-all | bytes 16384 | tf_op jit(solution)/shard_map/all_to_all | solution.py:331
  56.6 1.2 %shard_map.105 = (bf16[256,512]{1,0:T(8,128)(2,1)S(1)}, f32[768,128]{1,0:T(8,128)}) custom-call(bf16[512,256]{1,0:T(8,128)(2,1)S(1)} %get-tuple-element.25.turned_ref, f32[256,512]{1,0:T(8,128)S(1)} %get-tuple-element.29.att_ref, bf16[256,512]{1,0:T(8,128)(2,1)S(1)} %bitcast.36, f32[1,512]{1,0:T(1,128)S(1)} %bitcast.43, f32[16,128]{1,0:T(8,128)S(1)} %bitcast.39), custom_call_target="tpu_custom_call" | custom-call | flops 35651584 | bytes 1048576 | tf_op jit(solution)/shard_map/pallas_call | solution.py:249
  57.8 11.9 %all-to-all-start.3 = ((f32[64,3,4,128]{3,2,1,0:T(4,128)}), f32[64,3,4,128]{3,2,1,0:T(4,128)S(1)}, u32[]{:S(2)}, u32[]{:S(2)}) async-start(f32[64,3,4,128]{3,2,1,0:T(4,128)} %bitcast.13), calls=%async_computation.3 | async-start | bytes 786432 | tf_op jit(solution)/shard_map/all_to_all | solution.py:266
  69.7 2.9 %shard_map.106 = (bf16[256,512]{1,0:T(8,128)(2,1)}, f32[256,512]{1,0:T(8,128)S(1)}, f32[256,512]{1,0:T(8,128)S(1)}, bf16[256,512]{1,0:T(8,128)(2,1)}, f32[8,128]{1,0:T(8,128)S(1)}) custom-call(s32[1,4]{1,0:T(1,128)S(1)} %copy-done.5, bf16[256,512]{1,0:T(8,128)(2,1)S(1)} %bitcast.32, bf16[256,512]{1,0:T(8,128)(2,1)S(1)} %bitcast.22, ...), custom_call_target="tpu_custom_call" | custom-call | flops 356515840 | bytes 3145728 | tf_op jit(solution)/shard_map/pallas_call | solution.py:249
  72.7 5.4 %all-to-all-done.3 = f32[64,3,4,128]{3,2,1,0:T(4,128)S(1)} async-done(((f32[64,3,4,128]{3,2,1,0:T(4,128)}), f32[64,3,4,128]{3,2,1,0:T(4,128)S(1)}, u32[]{:S(2)}, u32[]{:S(2)}) %all-to-all-start.3) | async-done | bytes 393248 | tf_op jit(solution)/shard_map/all_to_all | solution.py:266
  78.1 0.8 shard_map.107
  78.9 11.8 %all-to-all-start.4 = ((f32[64,8,128]{2,1,0:T(8,128)}), f32[64,8,128]{2,1,0:T(8,128)S(1)}, u32[]{:S(2)}, u32[]{:S(2)}) async-start(f32[64,8,128]{2,1,0:T(8,128)} %bitcast.15), calls=%async_computation.4 | async-start | bytes 524288 | tf_op jit(solution)/shard_map/all_to_all | solution.py:266
  90.8 1.9 %collective-permute-start = (f32[4,128]{1,0:T(4,128)S(1)}, f32[4,128]{1,0:T(4,128)S(1)}, u32[]{:S(2)}, u32[]{:S(2)}) collective-permute-start(f32[4,128]{1,0:T(4,128)S(1)} %shard_map.108.part_ref), channel_id=1, source_target_pairs={{0,256},{256,0},{1,257},{257,1},{2,258},{258,2},{3,259},{259,3},{4... | collective-permute-start | bytes 6152 | tf_op jit(solution)/shard_map/ppermute | solution.py:372
  92.7 1.1 %collective-permute-done.other_ref = f32[4,128]{1,0:T(4,128)S(1)} collective-permute-done((f32[4,128]{1,0:T(4,128)S(1)}, f32[4,128]{1,0:T(4,128)S(1)}, u32[]{:S(2)}, u32[]{:S(2)}) %collective-permute-start) | collective-permute-done | bytes 2080 | tf_op jit(solution)/shard_map/ppermute | solution.py:372
  93.8 2.7 %all-to-all-done.4 = f32[64,8,128]{2,1,0:T(8,128)S(1)} async-done(((f32[64,8,128]{2,1,0:T(8,128)}), f32[64,8,128]{2,1,0:T(8,128)S(1)}, u32[]{:S(2)}, u32[]{:S(2)}) %all-to-all-start.4) | async-done | bytes 262176 | tf_op jit(solution)/shard_map/all_to_all | solution.py:266
  96.5 1.6 %shard_map.109 = (bf16[256,512]{1,0:T(8,128)(2,1)}, bf16[256,512]{1,0:T(8,128)(2,1)}, f32[4,128]{1,0:T(4,128)}) custom-call(s32[1,4]{1,0:T(1,128)S(1)} %copy-done.5, bf16[256,512]{1,0:T(8,128)(2,1)S(1)} %bitcast.23, bf16[256,512]{1,0:T(8,128)(2,1)S(1)} %bitcast.27, f32[512,128]{1,0:T(8,128)S(1)} %bitcast.37, f32[256,512]{1,0:T(8,128)S(1)} %get-tuple-element.39.gk_ref, ...), custom_call_target="tpu_custom_call" | custom-call | flops 71303168 | bytes 2097152 | tf_op jit(solution)/shard_map/pallas_call | solution.py:249
  (7 shorter events, 0.0 us)
Async XLA Ops:
  0.6 21.1 %copy-start.2 = (bf16[1,256,512]{2,1,0:T(8,128)(2,1)S(1)}, bf16[1,256,512]{2,1,0:T(8,128)(2,1)}, u32[]{:S(2)}) copy-start(bf16[1,256,512]{2,1,0:T(8,128)(2,1)} %param.6) | copy-start | bytes 786436
  2.7 19.0 %copy-start = (bf16[1,256,512]{2,1,0:T(8,128)(2,1)S(1)}, bf16[1,256,512]{2,1,0:T(8,128)(2,1)}, u32[]{:S(2)}) copy-start(bf16[1,256,512]{2,1,0:T(8,128)(2,1)} %param.7) | copy-start | bytes 786436
  2.7 19.0 %copy-start.1 = (bf16[1,256,512]{2,1,0:T(8,128)(2,1)S(1)}, bf16[1,256,512]{2,1,0:T(8,128)(2,1)}, u32[]{:S(2)}) copy-start(bf16[1,256,512]{2,1,0:T(8,128)(2,1)} %param.8) | copy-start | bytes 786436
  2.7 26.9 %all-to-all-start = ((f32[64,9,1,128]{3,2,1,0:T(1,128)}), f32[64,9,1,128]{3,2,1,0:T(1,128)S(1)}, u32[]{:S(2)}, u32[]{:S(2)}) async-start(f32[64,9,1,128]{3,2,1,0:T(1,128)} %bitcast.46), calls=%async_computation | async-start | bytes 589824 | tf_op jit(solution)/shard_map/all_to_all | solution.py:266
  21.7 0.7 copy-start.4
  21.7 0.7 copy-start.5
  29.7 18.3 %copy-start.3 = (bf16[1,256,512]{2,1,0:T(8,128)(2,1)S(1)}, bf16[1,256,512]{2,1,0:T(8,128)(2,1)}, u32[]{:S(2)}) copy-start(bf16[1,256,512]{2,1,0:T(8,128)(2,1)} %param.10) | copy-start | bytes 786436
  57.8 20.2 %all-to-all-start.3 = ((f32[64,3,4,128]{3,2,1,0:T(4,128)}), f32[64,3,4,128]{3,2,1,0:T(4,128)S(1)}, u32[]{:S(2)}, u32[]{:S(2)}) async-start(f32[64,3,4,128]{3,2,1,0:T(4,128)} %bitcast.13), calls=%async_computation.3 | async-start | bytes 786432 | tf_op jit(solution)/shard_map/all_to_all | solution.py:266
  78.9 17.6 %all-to-all-start.4 = ((f32[64,8,128]{2,1,0:T(8,128)}), f32[64,8,128]{2,1,0:T(8,128)S(1)}, u32[]{:S(2)}, u32[]{:S(2)}) async-start(f32[64,8,128]{2,1,0:T(8,128)} %bitcast.15), calls=%async_computation.4 | async-start | bytes 524288 | tf_op jit(solution)/shard_map/all_to_all | solution.py:266
  90.8 3.1 %collective-permute-start = (f32[4,128]{1,0:T(4,128)S(1)}, f32[4,128]{1,0:T(4,128)S(1)}, u32[]{:S(2)}, u32[]{:S(2)}) collective-permute-start(f32[4,128]{1,0:T(4,128)S(1)} %shard_map.108.part_ref), channel_id=1, source_target_pairs={{0,256},{256,0},{1,257},{257,1},{2,258},{258,2},{3,259},{259,3},{4... | collective-permute-start | bytes 6152 | tf_op jit(solution)/shard_map/ppermute | solution.py:372

commit v6 on v5

--- a/solution.py
+++ b/solution.py
@@ -93,10 +93,13 @@
         copy.wait()
 
 
-def local_kernel(off_ref, q_ref, k_ref, v_ref, gain_ref, out_ref, turned_ref, token_ref):
+def local_kernel(
+    off_ref, q_ref, k_ref, v_ref, gain_ref, out_ref, turned_ref, open_ref, token_ref
+):
     length, width = q_ref.shape
     first, _, _ = bounds(off_ref)
     opened = row_mask(length, first=first)
+    open_ref[...] = jnp.where(opened, 1.0, 0.0)
     allowed = allowed_of(off_ref, length)
     for h in range(width // DH):
         scores = dot(q_ref[:, head(h)], k_ref[:, head(h)], 1, 1)
@@ -132,18 +135,17 @@
 
 
 def attend_kernel(
-    off_ref, q_ref, local_ref, state_ref, g_ref, gain_ref, att_ref, sums_ref, carried_ref
+    open_ref, q_ref, local_ref, state_ref, g_ref, gain_ref, att_ref, sums_ref, carried_ref
 ):
     length, width = q_ref.shape
-    first, _, _ = bounds(off_ref)
-    opened = row_mask(length, first=first)
+    opened = open_ref[...]
     squares = jnp.zeros((length, DH), F32)
     products = jnp.zeros((length, DH), F32)
     for h in range(width // DH):
         carried = state_ref[h * DH : (h + 1) * DH, :].astype(BF16)
         carried_ref[h * DH : (h + 1) * DH, :] = carried
         carried_out = dot(q_ref[:, head(h)], carried, 1, 0)
-        att = local_ref[:, head(h)] + jnp.where(opened, carried_out, 0.0)
+        att = local_ref[:, head(h)] + opened * carried_out
         att_ref[:, head(h)] = att
         squares += att * att
         products += (gain_ref[:, head(h)] * g_ref[:, head(h)].astype(F32)) * att
@@ -207,12 +209,13 @@
 
 def grads_kernel(
     off_ref, q_ref, k_ref, v_ref, pre_ref, carried_ref, att_ref, gain_ref, sums_ref,
-    gq_ref, gk_ref, gv_ref, out_ref, token_ref,
+    gq_ref, gk_ref, gv_ref, out_ref, tail_ref, token_ref,
 ):
     length, width = q_ref.shape
     inverse, _ = columns_of(sums_ref, length)
     token_ref[...] = jnp.zeros_like(token_ref)
-    first, _, _ = bounds(off_ref)
+    first, last, _ = bounds(off_ref)
+    tail_ref[...] = jnp.where(row_mask(length, last=last), 1.0, 0.0)
     opened = row_mask(length, first=first)
     allowed = allowed_of(off_ref, length)
     for h in range(width // DH):
@@ -230,17 +233,16 @@
 
 
 def final_kernel(
-    off_ref, k_ref, v_ref, later_ref, gk_ref, gv_ref, part_ref, other_ref,
+    tail_ref, k_ref, v_ref, later_ref, gk_ref, gv_ref, part_ref, other_ref,
     outk_ref, outv_ref, gain_ref,
 ):
-    length, width = k_ref.shape
-    _, last, _ = bounds(off_ref)
-    tail = row_mask(length, last=last)
+    width = k_ref.shape[1]
+    tail = tail_ref[...]
     gain_ref[...] = part_ref[...] + other_ref[...]
     for h in range(width // DH):
         later = later_ref[h * DH : (h + 1) * DH, :].astype(BF16)
-        from_values = jnp.where(tail, dot(v_ref[:, head(h)], later, 1, 1), 0.0)
-        from_keys = jnp.where(tail, dot(k_ref[:, head(h)], later, 1, 0), 0.0)
+        from_values = tail * dot(v_ref[:, head(h)], later, 1, 1)
+        from_keys = tail * dot(k_ref[:, head(h)], later, 1, 0)
         outk_ref[:, head(h)] = (gk_ref[:, head(h)] + from_values).astype(BF16)
         outv_ref[:, head(h)] = (gv_ref[:, head(h)] + from_keys).astype(BF16)
 
@@ -301,9 +303,9 @@
     )
     tails = exchanged(tails, 9)
     token = (8, DH)
-    local, turned, ready = call(
+    local, turned, opened, ready = call(
         local_kernel,
-        [(wide, F32), ((width, length), BF16), (token, F32)],
+        [(wide, F32), ((width, length), BF16), ((length, DH), F32), (token, F32)],
         134 * mega,
         mega,
         off,
@@ -321,7 +323,7 @@
         [(wide, F32), ((16, DH), F32), ((width, DH), BF16)],
         34 * mega,
         mega,
-        off,
+        opened,
         q,
         local,
         state,
@@ -343,9 +345,16 @@
         sums,
     )
     grad_states = exchanged(grad_states, 12)
-    gq, gk, gv, out, ready = call(
+    gq, gk, gv, out, tail, ready = call(
         grads_kernel,
-        [(wide, BF16), (wide, F32), (wide, F32), (wide, BF16), (token, F32)],
+        [
+            (wide, BF16),
+            (wide, F32),
+            (wide, F32),
+            (wide, BF16),
+            ((length, DH), F32),
+            (token, F32),
+        ],
         340 * mega,
         3 * mega,
         off,
@@ -375,7 +384,7 @@
         [(wide, BF16), (wide, BF16), ((heads, DH), F32)],
         68 * mega,
         2 * mega,
-        off,
+        tail,
         k,
         v,
         later,

time: 98.6 us -> 97.5 us (0.989)
  Pallas kernels: 10.9 us -> 9.81 us
    pallas_call x9, Pallas kernels: 10.9 us -> 9.81 us  [call(): pl.pallas_call(kernel, out_shape=[jax.ShapeDtypeStruct(s, d) for s, d in...]
where the time goes in v6:
time: 97.5 us; the launch traced here: 97 us
  starting transfers between devices  44.6 us (46%)
  blocking collectives  26 us (27%)
  waiting for transfers between devices  15.2 us (16%)
  Pallas kernels  9.81 us (10%)
    all_to_all x3, starting transfers between devices, exchanged(): lax.all_to_all(rows.reshape((count, *tile, DH)), 'seq', 0, 0, axis_index_...  42.7 us
    all_to_all x1, blocking collectives, exchanged(): lax.all_to_all(rows.reshape((count, *tile, DH)), 'seq', 0, 0, axis_index_...  18.3 us
    all_to_all x3, waiting for transfers between devices, exchanged(): lax.all_to_all(rows.reshape((count, *tile, DH)), 'seq', 0, 0, axis_index_...  14.1 us
    pallas_call x9, Pallas kernels, call(): pl.pallas_call(kernel, out_shape=[jax.ShapeDtypeStruct(s, d) for s, d in...  9.81 us
    all_to_all x1, blocking collectives, shards(): lax.all_to_all(sums.reshape(4, 4, DH), 'tensor', 0, 0, axis_index_groups=...  7.69 us
  transfers between devices with their start and end apart: 4, of which 4 were waited for; matrix products, arithmetic and copies ran while one was open for 0% of the time, Pallas kernels for 4%

profile of v6, /device:TPU:2, one launch (start us, length us, event | category | flops | bytes accessed | tf_op | source)
XLA Modules:
  0.0 97.0 jit_solution(12918549987397225495)
XLA Ops:
  0.6 2.1 %shard_map.102 = f32[576,128]{1,0:T(8,128)} custom-call(s32[1,4]{1,0:T(1,128)} %off_ref.3, bf16[256,512]{1,0:T(8,128)(2,1)} %bitcast.20, bf16[256,512]{1,0:T(8,128)(2,1)} %bitcast.24), custom_call_target="tpu_custom_call" | custom-call | flops 35651584 | bytes 1048576 | tf_op jit(solution)/shard_map/pallas_call | solution.py:251
  2.7 0.0 copy-start
  2.7 0.0 copy-start.1
  2.7 19.0 %all-to-all-start = ((f32[64,9,1,128]{3,2,1,0:T(1,128)}), f32[64,9,1,128]{3,2,1,0:T(1,128)S(1)}, u32[]{:S(2)}, u32[]{:S(2)}) async-start(f32[64,9,1,128]{3,2,1,0:T(1,128)} %bitcast.46), calls=%async_computation | async-start | bytes 589824 | tf_op jit(solution)/shard_map/all_to_all | solution.py:268
  21.7 0.0 copy-start.4
  21.7 0.0 copy-start.5
  21.7 0.0 copy-done.2
  21.8 0.6 copy-done.4
  22.4 1.2 %shard_map.101 = (f32[256,512]{1,0:T(8,128)S(1)}, bf16[512,256]{1,0:T(8,128)(2,1)S(1)}, f32[256,128]{1,0:T(8,128)S(1)}, f32[8,128]{1,0:T(8,128)S(1)}) custom-call(s32[1,4]{1,0:T(1,128)S(1)} %copy-done.5, bf16[256,512]{1,0:T(8,128)(2,1)S(1)} %bitcast.30, bf16[256,512]{1,0:T(8,128)(2,1)S(1)} %bitcast.21, bf16[256,512]{1,0:T(8,128)(2,1)S(1)} %bitcast.25, ...), custom_call_target="tpu_custom_call" | custom-call | flops 140509184 | bytes 1048576 | tf_op jit(solution)/shard_map/pallas_call | solution.py:251
  23.6 6.0 %all-to-all-done = f32[64,9,1,128]{3,2,1,0:T(1,128)S(1)} async-done(((f32[64,9,1,128]{3,2,1,0:T(1,128)}), f32[64,9,1,128]{3,2,1,0:T(1,128)S(1)}, u32[]{:S(2)}, u32[]{:S(2)}) %all-to-all-start) | async-done | bytes 294944 | tf_op jit(solution)/shard_map/all_to_all | solution.py:268
  29.6 0.1 shard_map.103
  29.7 18.3 %all_to_all.25 = f32[64,8,128]{2,1,0:T(8,128)S(1)} all-to-all(f32[64,8,128]{2,1,0:T(8,128)S(1)} %bitcast.38), channel_id=1, replica_groups={{148,4,0,8,36,228,12,28,32,40,68,196,224,232,16,24,44,60,64,72,100,164,..., dimensions={0} | all-to-all | bytes 524288 | tf_op jit(solution)/shard_map/all_to_all | solution.py:268
  48.0 0.4 shard_map.104
  48.4 7.7 %all_to_all.26 = f32[4,4,128]{2,1,0:T(4,128)S(1)} all-to-all(f32[4,4,128]{2,1,0:T(4,128)S(1)} %bitcast.45), channel_id=1, replica_groups={{2,3,1,0},{6,7,5,4},{10,11,9,8},{14,15,13,12},{18,19,17,16},{22,23,21,2..., dimensions={0} | all-to-all | bytes 16384 | tf_op jit(solution)/shard_map/all_to_all | solution.py:333
  56.1 1.2 %shard_map.105 = (bf16[256,512]{1,0:T(8,128)(2,1)S(1)}, f32[768,128]{1,0:T(8,128)}) custom-call(bf16[512,256]{1,0:T(8,128)(2,1)S(1)} %get-tuple-element.27.turned_ref, f32[256,512]{1,0:T(8,128)S(1)} %get-tuple-element.32.att_ref, bf16[256,512]{1,0:T(8,128)(2,1)S(1)} %bitcast.37, f32[1,512]{1,0:T(1,128)S(1)} %bitcast.43, f32[16,128]{1,0:T(8,128)S(1)} %bitcast.39), custom_call_target="tpu_custom_call" | custom-call | flops 35651584 | bytes 1048576 | tf_op jit(solution)/shard_map/pallas_call | solution.py:251
  57.3 11.9 %all-to-all-start.3 = ((f32[64,3,4,128]{3,2,1,0:T(4,128)}), f32[64,3,4,128]{3,2,1,0:T(4,128)S(1)}, u32[]{:S(2)}, u32[]{:S(2)}) async-start(f32[64,3,4,128]{3,2,1,0:T(4,128)} %bitcast.13), calls=%async_computation.3 | async-start | bytes 786432 | tf_op jit(solution)/shard_map/all_to_all | solution.py:268
  69.2 2.9 %shard_map.106 = (bf16[256,512]{1,0:T(8,128)(2,1)}, f32[256,512]{1,0:T(8,128)S(1)}, f32[256,512]{1,0:T(8,128)S(1)}, bf16[256,512]{1,0:T(8,128)(2,1)}, f32[256,128]{1,0:T(8,128)S(1)}, /*index=5*/f32[8,128]{1,0:T(8,128)S(1)}) custom-call(s32[1,4]{1,0:T(1,128)S(1)} %copy-done.5, bf16[256,512]{1,0:T(8,128)(2,1)S(1)} %bitcast.32, bf16[256,512]{1,0:T(8,128)(2,1)S(1)} %bitcast.22, ...), custom_call_target="tpu_custom_call" | custom-call | flops 356515840 | bytes 3145728 | tf_op jit(solution)/shard_map/pallas_call | solution.py:251
  72.1 5.4 %all-to-all-done.3 = f32[64,3,4,128]{3,2,1,0:T(4,128)S(1)} async-done(((f32[64,3,4,128]{3,2,1,0:T(4,128)}), f32[64,3,4,128]{3,2,1,0:T(4,128)S(1)}, u32[]{:S(2)}, u32[]{:S(2)}) %all-to-all-start.3) | async-done | bytes 393248 | tf_op jit(solution)/shard_map/all_to_all | solution.py:268
  77.5 0.8 shard_map.107
  78.4 11.8 %all-to-all-start.4 = ((f32[64,8,128]{2,1,0:T(8,128)}), f32[64,8,128]{2,1,0:T(8,128)S(1)}, u32[]{:S(2)}, u32[]{:S(2)}) async-start(f32[64,8,128]{2,1,0:T(8,128)} %bitcast.15), calls=%async_computation.4 | async-start | bytes 524288 | tf_op jit(solution)/shard_map/all_to_all | solution.py:268
  90.2 1.9 %collective-permute-start = (f32[4,128]{1,0:T(4,128)S(1)}, f32[4,128]{1,0:T(4,128)S(1)}, u32[]{:S(2)}, u32[]{:S(2)}) collective-permute-start(f32[4,128]{1,0:T(4,128)S(1)} %shard_map.108.part_ref), channel_id=1, source_target_pairs={{0,256},{256,0},{1,257},{257,1},{2,258},{258,2},{3,259},{259,3},{4... | collective-permute-start | bytes 6152 | tf_op jit(solution)/shard_map/ppermute | solution.py:381
  92.1 1.1 %collective-permute-done.other_ref = f32[4,128]{1,0:T(4,128)S(1)} collective-permute-done((f32[4,128]{1,0:T(4,128)S(1)}, f32[4,128]{1,0:T(4,128)S(1)}, u32[]{:S(2)}, u32[]{:S(2)}) %collective-permute-start) | collective-permute-done | bytes 2080 | tf_op jit(solution)/shard_map/ppermute | solution.py:381
  93.3 2.7 %all-to-all-done.4 = f32[64,8,128]{2,1,0:T(8,128)S(1)} async-done(((f32[64,8,128]{2,1,0:T(8,128)}), f32[64,8,128]{2,1,0:T(8,128)S(1)}, u32[]{:S(2)}, u32[]{:S(2)}) %all-to-all-start.4) | async-done | bytes 262176 | tf_op jit(solution)/shard_map/all_to_all | solution.py:268
  96.0 1.1 %shard_map.109 = (bf16[256,512]{1,0:T(8,128)(2,1)}, bf16[256,512]{1,0:T(8,128)(2,1)}, f32[4,128]{1,0:T(4,128)}) custom-call(f32[256,128]{1,0:T(8,128)S(1)} %get-tuple-element.38.tail_ref, bf16[256,512]{1,0:T(8,128)(2,1)S(1)} %bitcast.23, bf16[256,512]{1,0:T(8,128)(2,1)S(1)} %bitcast.27, f32[512,128]{1,0:T(8,128)S(1)} %bitcast.34, ...), custom_call_target="tpu_custom_call" | custom-call | flops 71303168 | bytes 2097152 | tf_op jit(solution)/shard_map/pallas_call | solution.py:251
  (7 shorter events, 0.0 us)
Async XLA Ops:
  0.6 21.1 %copy-start.2 = (bf16[1,256,512]{2,1,0:T(8,128)(2,1)S(1)}, bf16[1,256,512]{2,1,0:T(8,128)(2,1)}, u32[]{:S(2)}) copy-start(bf16[1,256,512]{2,1,0:T(8,128)(2,1)} %param.6) | copy-start | bytes 786436
  2.7 19.0 %copy-start = (bf16[1,256,512]{2,1,0:T(8,128)(2,1)S(1)}, bf16[1,256,512]{2,1,0:T(8,128)(2,1)}, u32[]{:S(2)}) copy-start(bf16[1,256,512]{2,1,0:T(8,128)(2,1)} %param.7) | copy-start | bytes 786436
  2.7 19.0 %copy-start.1 = (bf16[1,256,512]{2,1,0:T(8,128)(2,1)S(1)}, bf16[1,256,512]{2,1,0:T(8,128)(2,1)}, u32[]{:S(2)}) copy-start(bf16[1,256,512]{2,1,0:T(8,128)(2,1)} %param.8) | copy-start | bytes 786436
  2.7 26.9 %all-to-all-start = ((f32[64,9,1,128]{3,2,1,0:T(1,128)}), f32[64,9,1,128]{3,2,1,0:T(1,128)S(1)}, u32[]{:S(2)}, u32[]{:S(2)}) async-start(f32[64,9,1,128]{3,2,1,0:T(1,128)} %bitcast.46), calls=%async_computation | async-start | bytes 589824 | tf_op jit(solution)/shard_map/all_to_all | solution.py:268
  21.7 0.7 copy-start.4
  21.7 0.7 copy-start.5
  29.7 18.3 %copy-start.3 = (bf16[1,256,512]{2,1,0:T(8,128)(2,1)S(1)}, bf16[1,256,512]{2,1,0:T(8,128)(2,1)}, u32[]{:S(2)}) copy-start(bf16[1,256,512]{2,1,0:T(8,128)(2,1)} %param.10) | copy-start | bytes 786436
  57.3 20.2 %all-to-all-start.3 = ((f32[64,3,4,128]{3,2,1,0:T(4,128)}), f32[64,3,4,128]{3,2,1,0:T(4,128)S(1)}, u32[]{:S(2)}, u32[]{:S(2)}) async-start(f32[64,3,4,128]{3,2,1,0:T(4,128)} %bitcast.13), calls=%async_computation.3 | async-start | bytes 786432 | tf_op jit(solution)/shard_map/all_to_all | solution.py:268
  78.4 17.6 %all-to-all-start.4 = ((f32[64,8,128]{2,1,0:T(8,128)}), f32[64,8,128]{2,1,0:T(8,128)S(1)}, u32[]{:S(2)}, u32[]{:S(2)}) async-start(f32[64,8,128]{2,1,0:T(8,128)} %bitcast.15), calls=%async_computation.4 | async-start | bytes 524288 | tf_op jit(solution)/shard_map/all_to_all | solution.py:268
  90.2 3.1 %collective-permute-start = (f32[4,128]{1,0:T(4,128)S(1)}, f32[4,128]{1,0:T(4,128)S(1)}, u32[]{:S(2)}, u32[]{:S(2)}) collective-permute-start(f32[4,128]{1,0:T(4,128)S(1)} %shard_map.108.part_ref), channel_id=1, source_target_pairs={{0,256},{256,0},{1,257},{257,1},{2,258},{258,2},{3,259},{259,3},{4... | collective-permute-start | bytes 6152 | tf_op jit(solution)/shard_map/ppermute | solution.py:381
